TPU v7x, 32 devices: a whole 2x2x4 slice. The times are simulated.
32 devices in a mesh: fsdp: 16 (over z, x, core), seq: 2 (over y).
Axes of the slice: x: 2, y: 2, z: 4, core: 2. Of those that a mesh axis runs over, the one named last changes fastest.
Arguments:
- stream: float32 [16, 256, 768], P('fsdp', 'seq'), may hold values from -24 to 24
- encoder: bfloat16 [16, 64, 768], P('fsdp', 'seq'), may hold values from -6 to 6
- self_weights: bfloat16 [3072, 768], P('fsdp'), may hold values from -2 to 2
- cross_weights: bfloat16 [3072, 768], P('fsdp'), may hold values from -2 to 2
- feed_weights: bfloat16 [6144, 768], P('fsdp'), may hold values from -2 to 2
- norm_gains: bfloat16 [3, 768], P(None, 'fsdp'), may hold values from 0.5 to 1.5
- bias_table: float32 [12, 32], replicated, may hold values from -6 to 403
- bucket_onehot: int32 [256, 32], replicated, may hold values from 0 to 1, as said below
- key_keep: int32 [16, 256], P('fsdp'), may hold values 0 or 1
- out_grad: float32 [16, 256, 768], P('fsdp', 'seq'), may hold values from -6 to 6
Outputs:
- output: float32 [16, 256, 768], P('fsdp', 'seq')
- stream_grad: float32 [16, 256, 768], P('fsdp', 'seq')
- encoder_grad: float32 [16, 64, 768], P('fsdp', 'seq')
- gains_grad: float32 [3, 768], replicated
- table_grad: float32 [12, 32], replicated
- self_grad: float32 [3072, 768], P(('fsdp', 'seq'))
- cross_grad: float32 [3072, 768], P(('fsdp', 'seq'))
- feed_grad: float32 [6144, 768], P(('fsdp', 'seq'))
Inputs may be any that keep to these rules, and one draw needn't show every extreme that they name: `bucket_onehot`: row r holds a single 1, at the bucket of distance r; bucket numbers never fall as r grows.
All inputs are finite; a program needn't handle non-finite values. No bound on the sum of `key_keep` on one device may be relied on, other than what follows from the above.
Results may differ from a plain program's by a relative error of at most 0.017.
The roundings to bfloat16 on the way count: a program that leaves them out, or rounds other values in their place, can miss the bound.
Values may be sent and summed in bfloat16 or wider, within the bound.
No kernel may reach another device: no remote copies, remote signals or barrier semaphores. Data moves between devices by JAX's collectives and lax.ppermute only.
A program may use at most 128 MiB of HBM per device.

v0:
```python
import math

import jax
import jax.numpy as jnp
from jax import lax
from jax.sharding import PartitionSpec as P

H = 12
DK = 64
F = 2048


epsilon = 1e-06
gelu_scale = math.sqrt(2.0 / math.pi)


def rms_norm(rows, gain):
    scale = lax.rsqrt(jnp.mean(rows * rows, axis=-1) + epsilon)
    return ((rows * scale[:, None] * gain).astype(jnp.bfloat16), scale)


def norm_back(rows, scale, gain, dnorm):
    gained = gain * dnorm
    inner = jnp.mean(rows * gained, axis=-1, keepdims=True)
    drows = scale[:, None] * gained - rows * (scale**3)[:, None] * inner
    dgain = jnp.sum(dnorm * rows * scale[:, None], axis=0)
    return (drows, dgain)


def gelu_parts(value):
    tangent = jnp.tanh(gelu_scale * (value + 0.044715 * value * value * value))
    result = 0.5 * value * (1.0 + tangent)
    slope = 0.5 * (1.0 + tangent) + 0.5 * value * (1.0 - tangent * tangent) * gelu_scale * (
        1.0 + 3.0 * 0.044715 * value * value
    )
    return (result, slope)


def contract_rows(left, right):
    return lax.dot_general(
        left, right, (((0,), (0,)), ((), ())), preferred_element_type=jnp.float32
    )


def contract_cols(left, right):
    return lax.dot_general(
        left, right, (((1,), (1,)), ((), ())), preferred_element_type=jnp.float32
    )


def project(rows, stack, which, features):
    return jnp.dot(
        rows, stack[which * features : (which + 1) * features], preferred_element_type=jnp.float32
    ).astype(jnp.bfloat16)


def split_heads(values):
    return values.reshape(values.shape[0], values.shape[1], -1, DK)


def merge_heads(values):
    return values.reshape(values.shape[0], values.shape[1], -1)


def flatten_rows(values):
    return values.reshape(values.shape[0] * values.shape[1], values.shape[2])


def skew_bias(dist_bias, first_row, block_rows):
    key_end = first_row + block_rows
    line_len = key_end + block_rows - 1
    front_part = jnp.flip(dist_bias[:, : first_row + 1], axis=1)
    gap_zeros = jnp.zeros((dist_bias.shape[0], block_rows - 1), jnp.float32)
    back_part = jnp.flip(dist_bias[:, first_row + 1 : key_end], axis=1)
    diag_line = jnp.concatenate([front_part, gap_zeros, back_part], axis=1)
    tiled_line = jnp.tile(diag_line, (1, block_rows))[:, : block_rows * (line_len - 1)]
    return tiled_line.reshape(dist_bias.shape[0], block_rows, line_len - 1)[:, :, :key_end]


def skew_back(score_sum, first_row, block_rows):
    key_end = first_row + block_rows
    line_len = key_end + block_rows - 1
    head_count = score_sum.shape[0]
    padded = jnp.pad(score_sum, ((0, 0), (0, 0), (0, line_len - 1 - key_end)))
    flat_rows = jnp.pad(
        padded.reshape(head_count, block_rows * (line_len - 1)), ((0, 0), (0, block_rows))
    )
    diag_line = jnp.sum(flat_rows.reshape(head_count, block_rows, line_len), axis=1)
    near_part = jnp.flip(diag_line[:, : first_row + 1], axis=1)
    far_part = jnp.flip(diag_line[:, key_end:], axis=1)
    return jnp.concatenate([near_part, far_part], axis=1)


def block_scores(query_heads, key_heads, first_row, block_rows, causal_setup):
    key_end = first_row + block_rows if causal_setup is not None else key_heads.shape[1]
    query_block = split_heads(query_heads)
    key_block = split_heads(key_heads)
    scores = jnp.einsum(
        "sqhd,skhd->shqk", query_block, key_block, preferred_element_type=jnp.float32
    )
    if causal_setup is not None:
        dist_bias, keep_keys = causal_setup
        scores = scores + skew_bias(dist_bias, first_row, block_rows)[None]
        row_pos = first_row + jnp.arange(block_rows)[:, None]
        col_pos = jnp.arange(key_end)[None, :]
        allowed = (col_pos <= row_pos)[None, None] & (
            keep_keys[:, None, None, :key_end] | (col_pos == row_pos)[None, None]
        )
        scores = jnp.where(allowed, scores, -jnp.inf)
    return (scores, key_end)


def attend_forward(query_heads, key_heads, value_heads, block_rows, causal_setup):
    scores, key_end = block_scores(query_heads, key_heads, 0, block_rows, causal_setup)
    row_max = jnp.max(scores, axis=-1, keepdims=True)
    totals = row_max + jnp.log(jnp.sum(jnp.exp(scores - row_max), axis=-1, keepdims=True))
    attn_prob = jnp.exp(scores - totals).astype(jnp.bfloat16)
    value_block = split_heads(value_heads)
    context = jnp.einsum(
        "shqk,skhd->sqhd", attn_prob, value_block, preferred_element_type=jnp.float32
    )
    out_parts = merge_heads(context.astype(jnp.bfloat16))
    return (out_parts, totals)


def attend_backward(
    query_heads,
    key_heads,
    value_heads,
    context_heads,
    totals,
    grad_heads,
    block_rows,
    causal_setup,
    full_len,
):
    key_acc = jnp.zeros(split_heads(key_heads).shape, jnp.float32)
    value_acc = jnp.zeros(split_heads(value_heads).shape, jnp.float32)
    dist_grad = jnp.zeros((key_acc.shape[2], full_len), jnp.float32)
    scores, key_end = block_scores(query_heads, key_heads, 0, block_rows, causal_setup)
    attn_prob = jnp.exp(scores - totals)
    prob_low = attn_prob.astype(jnp.bfloat16)
    grad_block = split_heads(grad_heads)
    out_block = split_heads(context_heads)
    query_block = split_heads(query_heads)
    key_block = split_heads(key_heads)
    value_block = split_heads(value_heads)
    row_delta = jnp.einsum(
        "sqhd,sqhd->shq", out_block, grad_block, preferred_element_type=jnp.float32
    )[..., None]
    value_acc = value_acc.at[:, :key_end].add(
        jnp.einsum("shqk,sqhd->skhd", prob_low, grad_block, preferred_element_type=jnp.float32)
    )
    prob_grad = jnp.einsum(
        "sqhd,skhd->shqk", grad_block, value_block, preferred_element_type=jnp.float32
    )
    score_grad = attn_prob * (prob_grad - row_delta)
    if causal_setup is not None:
        dist_grad = skew_back(jnp.sum(score_grad, axis=0), 0, block_rows)
    score_low = score_grad.astype(jnp.bfloat16)
    query_grad = jnp.einsum(
        "shqk,skhd->sqhd", score_low, key_block, preferred_element_type=jnp.float32
    )
    query_parts = merge_heads(query_grad.astype(jnp.bfloat16))
    key_acc = key_acc.at[:, :key_end].add(
        jnp.einsum("shqk,sqhd->skhd", score_low, query_block, preferred_element_type=jnp.float32)
    )
    return (
        query_parts,
        merge_heads(key_acc).astype(jnp.bfloat16),
        merge_heads(value_acc).astype(jnp.bfloat16),
        dist_grad,
    )


def local(
    stream,
    encoder,
    self_weights,
    cross_weights,
    feed_weights,
    norm_gains,
    bias_table,
    bucket_onehot,
    key_keep,
    out_grad,
):
    group_size = lax.axis_size("seq")
    group_index = lax.axis_index("seq")
    seq_count, piece_len, features = stream.shape
    enc_piece = encoder.shape[1]
    full_len = piece_len * group_size
    local_heads = H // group_size
    head_cols = features // group_size
    token_count = seq_count * piece_len
    block_rows = min(512, full_len)
    bucket_count = bucket_onehot.shape[1]

    def attn_gather():
        return (
            lax.all_gather(self_weights, "fsdp", axis=0, tiled=True),
            lax.all_gather(cross_weights, "fsdp", axis=0, tiled=True),
            lax.all_gather(norm_gains, "fsdp", axis=1, tiled=True),
        )

    def feed_gather():
        return lax.all_gather(feed_weights, "fsdp", axis=0, tiled=True)

    self_full, cross_full, gains_full = attn_gather()
    gain_rows = gains_full.astype(jnp.float32)
    flat_stream = stream.reshape(token_count, features)
    norm_one, scale_one = rms_norm(flat_stream, gain_rows[0])
    queries = project(norm_one, self_full, 0, features).reshape(seq_count, piece_len, features)
    key_rows = project(norm_one, self_full, 1, features).reshape(seq_count, piece_len, features)
    value_rows = project(norm_one, self_full, 2, features).reshape(seq_count, piece_len, features)
    query_heads, key_heads, value_heads = (
        lax.all_to_all(queries, "seq", split_axis=2, concat_axis=1, tiled=True),
        lax.all_to_all(key_rows, "seq", split_axis=2, concat_axis=1, tiled=True),
        lax.all_to_all(value_rows, "seq", split_axis=2, concat_axis=1, tiled=True),
    )
    table_rows = lax.dynamic_slice_in_dim(bias_table, group_index * local_heads, local_heads, 0)
    onehot = bucket_onehot.astype(jnp.float32)
    dist_bias = jnp.dot(table_rows, onehot.T, precision=lax.Precision.HIGHEST)
    causal_setup = (dist_bias, key_keep == 1)
    self_context_heads, self_totals = attend_forward(
        query_heads, key_heads, value_heads, block_rows, causal_setup
    )
    self_context = lax.all_to_all(
        self_context_heads, "seq", split_axis=1, concat_axis=2, tiled=True
    ).reshape(token_count, features)
    after_self = flat_stream + jnp.dot(
        self_context, self_full[3 * features :], preferred_element_type=jnp.float32
    )
    norm_two, scale_two = rms_norm(after_self, gain_rows[1])
    flat_encoder = encoder.reshape(seq_count * enc_piece, features)
    cross_queries = project(norm_two, cross_full, 0, features).reshape(
        seq_count, piece_len, features
    )
    cross_keys = project(flat_encoder, cross_full, 1, features).reshape(
        seq_count, enc_piece, features
    )
    cross_values = project(flat_encoder, cross_full, 2, features).reshape(
        seq_count, enc_piece, features
    )
    cq_heads, ck_heads, cv_heads = (
        lax.all_to_all(cross_queries, "seq", split_axis=2, concat_axis=1, tiled=True),
        lax.all_to_all(cross_keys, "seq", split_axis=2, concat_axis=1, tiled=True),
        lax.all_to_all(cross_values, "seq", split_axis=2, concat_axis=1, tiled=True),
    )
    cross_context_heads, cross_totals = attend_forward(
        cq_heads, ck_heads, cv_heads, block_rows, None
    )
    cross_context = lax.all_to_all(
        cross_context_heads, "seq", split_axis=1, concat_axis=2, tiled=True
    ).reshape(token_count, features)
    after_cross = after_self + jnp.dot(
        cross_context, cross_full[3 * features :], preferred_element_type=jnp.float32
    )
    feed_full = feed_gather()
    norm_three, scale_three = rms_norm(after_cross, gain_rows[2])
    gate_pre = contract_cols(norm_three, feed_full[:F])
    up_pre = contract_cols(norm_three, feed_full[F : 2 * F])
    gate_act, gate_slope = gelu_parts(gate_pre)
    hidden = (gate_act * up_pre).astype(jnp.bfloat16)
    output = after_cross + jnp.dot(hidden, feed_full[2 * F :], preferred_element_type=jnp.float32)
    feed_back = feed_gather()
    flat_cotangent = out_grad.reshape(token_count, features)
    cot_low = flat_cotangent.astype(jnp.bfloat16)
    hidden_grad = contract_cols(cot_low, feed_back[2 * F :])
    gate_grad = (hidden_grad * up_pre * gate_slope).astype(jnp.bfloat16)
    up_grad = (hidden_grad * gate_act).astype(jnp.bfloat16)
    norm_three_grad = jnp.dot(
        gate_grad, feed_back[:F], preferred_element_type=jnp.float32
    ) + jnp.dot(up_grad, feed_back[F : 2 * F], preferred_element_type=jnp.float32)
    self_back, cross_back, gains_back = attn_gather()
    back_gains = gains_back.astype(jnp.float32)
    stream_three, gain_three = norm_back(after_cross, scale_three, back_gains[2], norm_three_grad)
    cross_in_grad = flat_cotangent + stream_three
    cross_low = cross_in_grad.astype(jnp.bfloat16)
    cross_context_grad = contract_cols(cross_low, cross_back[3 * features :]).astype(jnp.bfloat16)
    cross_grad_heads = lax.all_to_all(
        cross_context_grad.reshape(seq_count, piece_len, features),
        "seq",
        split_axis=2,
        concat_axis=1,
        tiled=True,
    )
    cq_grad_heads, ck_grad_heads, cv_grad_heads, unused_grad = attend_backward(
        cq_heads,
        ck_heads,
        cv_heads,
        cross_context_heads,
        cross_totals,
        cross_grad_heads,
        block_rows,
        None,
        full_len,
    )
    cq_grad, ck_grad, cv_grad = (
        lax.all_to_all(cq_grad_heads, "seq", split_axis=1, concat_axis=2, tiled=True),
        lax.all_to_all(ck_grad_heads, "seq", split_axis=1, concat_axis=2, tiled=True),
        lax.all_to_all(cv_grad_heads, "seq", split_axis=1, concat_axis=2, tiled=True),
    )
    cq_grad = cq_grad.reshape(token_count, features)
    ck_grad = ck_grad.reshape(seq_count * enc_piece, features)
    cv_grad = cv_grad.reshape(seq_count * enc_piece, features)
    norm_two_grad = contract_cols(cq_grad, cross_back[:features])
    encoder_grad = contract_cols(ck_grad, cross_back[features : 2 * features]) + contract_cols(
        cv_grad, cross_back[2 * features : 3 * features]
    )
    stream_two, gain_two = norm_back(after_self, scale_two, back_gains[1], norm_two_grad)
    self_in_grad = cross_in_grad + stream_two
    self_low = self_in_grad.astype(jnp.bfloat16)
    self_context_grad = contract_cols(self_low, self_back[3 * features :]).astype(jnp.bfloat16)
    self_grad_heads = lax.all_to_all(
        self_context_grad.reshape(seq_count, piece_len, features),
        "seq",
        split_axis=2,
        concat_axis=1,
        tiled=True,
    )
    sq_grad_heads, sk_grad_heads, sv_grad_heads, dist_grad = attend_backward(
        query_heads,
        key_heads,
        value_heads,
        self_context_heads,
        self_totals,
        self_grad_heads,
        block_rows,
        causal_setup,
        full_len,
    )
    sq_grad, sk_grad, sv_grad = (
        lax.all_to_all(sq_grad_heads, "seq", split_axis=1, concat_axis=2, tiled=True),
        lax.all_to_all(sk_grad_heads, "seq", split_axis=1, concat_axis=2, tiled=True),
        lax.all_to_all(sv_grad_heads, "seq", split_axis=1, concat_axis=2, tiled=True),
    )
    sq_grad = sq_grad.reshape(token_count, features)
    sk_grad = sk_grad.reshape(token_count, features)
    sv_grad = sv_grad.reshape(token_count, features)
    norm_one_grad = (
        contract_cols(sq_grad, self_back[:features])
        + contract_cols(sk_grad, self_back[features : 2 * features])
        + contract_cols(sv_grad, self_back[2 * features : 3 * features])
    )
    stream_one, gain_one = norm_back(flat_stream, scale_one, back_gains[0], norm_one_grad)
    stream_grad = self_in_grad + stream_one
    table_local = jnp.dot(dist_grad, onehot, precision=lax.Precision.HIGHEST)
    table_full = lax.dynamic_update_slice(
        jnp.zeros((H, bucket_count), jnp.float32),
        table_local,
        (group_index * local_heads, jnp.zeros((), jnp.int32)),
    )
    gain_grads = jnp.stack([gain_one, gain_two, gain_three])
    gains_total, table_total = lax.psum((gain_grads, table_full), ("fsdp", "seq"))

    def as_pieces(values):
        return values.reshape(seq_count, -1, values.shape[-1])

    (
        norm_one_all,
        self_ctx_all,
        self_low_all,
        norm_two_all,
        cross_ctx_all,
        cross_low_all,
        encoder_all,
        norm_three_all,
        cot_all,
        gate_all,
        up_all,
        hidden_all,
    ) = (
        lax.all_gather(as_pieces(norm_one), "seq", axis=1, tiled=True),
        lax.all_gather(as_pieces(self_context), "seq", axis=1, tiled=True),
        lax.all_gather(as_pieces(self_low), "seq", axis=1, tiled=True),
        lax.all_gather(as_pieces(norm_two), "seq", axis=1, tiled=True),
        lax.all_gather(as_pieces(cross_context), "seq", axis=1, tiled=True),
        lax.all_gather(as_pieces(cross_low), "seq", axis=1, tiled=True),
        lax.all_gather(encoder, "seq", axis=1, tiled=True),
        lax.all_gather(as_pieces(norm_three), "seq", axis=1, tiled=True),
        lax.all_gather(as_pieces(cot_low), "seq", axis=1, tiled=True),
        lax.all_gather(as_pieces(gate_grad), "seq", axis=1, tiled=True),
        lax.all_gather(as_pieces(up_grad), "seq", axis=1, tiled=True),
        lax.all_gather(as_pieces(hidden), "seq", axis=1, tiled=True),
    )
    col_start = group_index * head_cols
    self_low_cols = flatten_rows(lax.dynamic_slice_in_dim(self_low_all, col_start, head_cols, 2))
    cross_low_cols = flatten_rows(lax.dynamic_slice_in_dim(cross_low_all, col_start, head_cols, 2))
    norm_three_cols = flatten_rows(
        lax.dynamic_slice_in_dim(norm_three_all, col_start, head_cols, 2)
    )
    cot_cols = flatten_rows(lax.dynamic_slice_in_dim(cot_all, col_start, head_cols, 2))
    norm_one_rows = flatten_rows(norm_one_all)
    norm_two_rows = flatten_rows(norm_two_all)
    encoder_rows = flatten_rows(encoder_all)
    self_slab = jnp.concatenate(
        [
            contract_rows(norm_one_rows, flatten_rows(sq_grad_heads)),
            contract_rows(norm_one_rows, flatten_rows(sk_grad_heads)),
            contract_rows(norm_one_rows, flatten_rows(sv_grad_heads)),
            contract_rows(flatten_rows(self_ctx_all), self_low_cols),
        ],
        axis=0,
    )
    cross_slab = jnp.concatenate(
        [
            contract_rows(norm_two_rows, flatten_rows(cq_grad_heads)),
            contract_rows(encoder_rows, flatten_rows(ck_grad_heads)),
            contract_rows(encoder_rows, flatten_rows(cv_grad_heads)),
            contract_rows(flatten_rows(cross_ctx_all), cross_low_cols),
        ],
        axis=0,
    )
    feed_slab = jnp.concatenate(
        [
            contract_rows(flatten_rows(gate_all), norm_three_cols),
            contract_rows(flatten_rows(up_all), norm_three_cols),
            contract_rows(flatten_rows(hidden_all), cot_cols),
        ],
        axis=0,
    )
    self_part, cross_part, feed_part = (
        lax.psum_scatter(self_slab, "fsdp", scatter_dimension=0, tiled=True),
        lax.psum_scatter(cross_slab, "fsdp", scatter_dimension=0, tiled=True),
        lax.psum_scatter(feed_slab, "fsdp", scatter_dimension=0, tiled=True),
    )
    self_share, cross_share, feed_share = (
        lax.all_to_all(
            self_part.astype(jnp.bfloat16), "seq", split_axis=0, concat_axis=1, tiled=True
        ).astype(self_part.dtype),
        lax.all_to_all(
            cross_part.astype(jnp.bfloat16), "seq", split_axis=0, concat_axis=1, tiled=True
        ).astype(cross_part.dtype),
        lax.all_to_all(
            feed_part.astype(jnp.bfloat16), "seq", split_axis=0, concat_axis=1, tiled=True
        ).astype(feed_part.dtype),
    )
    return (
        output.reshape(seq_count, piece_len, features),
        stream_grad.reshape(seq_count, piece_len, features),
        encoder_grad.reshape(seq_count, enc_piece, features),
        gains_total,
        table_total,
        self_share,
        cross_share,
        feed_share,
    )


def solution(mesh):
    placed = (
        P("fsdp", "seq", None),
        P("fsdp", "seq", None),
        P("fsdp", None),
        P("fsdp", None),
        P("fsdp", None),
        P(None, "fsdp"),
        P(),
        P(),
        P("fsdp", None),
        P("fsdp", "seq", None),
    )
    return jax.shard_map(
        local,
        mesh=mesh,
        in_specs=placed,
        out_specs=(
            P("fsdp", "seq", None),
            P("fsdp", "seq", None),
            P("fsdp", "seq", None),
            P(),
            P(),
            P(("fsdp", "seq"), None),
            P(("fsdp", "seq"), None),
            P(("fsdp", "seq"), None),
        ),
        check_vma=False,
    )
```

profile of v0, /device:TPU:0, one launch (start us, length us, event | category | flops | bytes accessed | tf_op | source)
XLA Modules:
  0.0 587.3 jit_solution(906610574249438284)
XLA Ops:
  10.4 23.5 %all-gather.7 = bf16[16,48,3]{1,2,0:T(4,128)(2,1)S(1)} all-gather(bf16[1,48,3]{1,2,0:T(4,128)(2,1)} %bitcast.413), channel_id=1, replica_groups=mesh['fsdp'=16,'seq'=2] {'fsdp'}, dimensions={0}, use_global_device_ids=true | all-gather | bytes 4896 | tf_op jit(solution)/shard_map/all_gather | solution.py:203
  35.3 4.8 tile.5
  40.1 4.6 slice.200
  44.6 5.3 reshape.712
  55.3 10.8 %all-gather.15.cloned.1.call-done = bf16[3072,768]{1,0:T(8,128)(2,1)} async-done(((bf16[192,768]{1,0:T(8,128)(2,1)}), bf16[3072,768]{1,0:T(8,128)(2,1)}) %all-gather.15.cloned.1.call-update) | async-done | bytes 4718608 | tf_op jit(solution)/shard_map/all_gather | solution.py:201
  71.3 3.4 all-to-all-start
  79.9 3.6 all-to-all-start.1
  88.3 3.4 all-to-all-start.2
  91.7 28.4 %all-gather.17.cloned.1.call-done = bf16[3072,768]{1,0:T(8,128)(2,1)} async-done(((bf16[192,768]{1,0:T(8,128)(2,1)}), bf16[3072,768]{1,0:T(8,128)(2,1)}) %all-gather.17.cloned.1.call-update) | async-done | bytes 4718608 | tf_op jit(solution)/shard_map/all_gather | solution.py:202
  134.8 3.4 all-to-all-start.3
  143.4 3.3 all-to-all-start.4
  150.7 3.3 all-to-all-start.6
  158.6 3.4 all-to-all-start.5
  169.2 3.4 reduce.35
  174.2 8.2 %all_to_all.285 = bf16[2,2,24576]{2,1,0:T(2,128)(2,1)S(1)} all-to-all(bf16[2,2,24576]{2,1,0:T(2,128)(2,1)} %reshape.811), channel_id=1, replica_groups=mesh['fsdp'=16,'seq'=2] {'seq'}, dimensions={0} | all-to-all | bytes 393216 | tf_op jit(solution)/shard_map/all_to_all | solution.py:253
  189.7 12.2 %all-gather.19.cloned.1.call-done = bf16[6144,768]{1,0:T(8,128)(2,1)} async-done(((bf16[384,768]{1,0:T(8,128)(2,1)}), bf16[6144,768]{1,0:T(8,128)(2,1)}) %all-gather.19.cloned.1.call-update) | async-done | bytes 9437200 | tf_op jit(solution)/shard_map/all_gather | solution.py:207
  208.0 4.7 fusion.39
  212.8 6.0 %all_gather.60 = bf16[1,64,768]{2,1,0:T(8,128)(2,1)} all-gather(bf16[1,32,768]{2,1,0:T(8,128)(2,1)} %param.27), channel_id=1, replica_groups=mesh['fsdp'=16,'seq'=2] {'seq'}, dimensions={1}, use_global_device_ids=true | all-gather | bytes 147456 | tf_op jit(solution)/shard_map/all_gather | solution.py:380
  218.8 12.6 %all-gather.1 = bf16[256,768]{1,0:T(8,128)(2,1)} all-gather(bf16[128,768]{1,0:T(8,128)(2,1)} %copy-done.37), channel_id=3, replica_groups=mesh['fsdp'=16,'seq'=2] {'seq'}, dimensions={0}, use_global_device_ids=true | all-gather | bytes 589824 | tf_op jit(solution)/shard_map/all_gather | solution.py:377
  231.4 9.5 %all_gather.61 = bf16[1,256,768]{1,2,0:T(8,128)(2,1)} all-gather(bf16[1,128,768]{1,2,0:T(8,128)(2,1)} %bitcast.336), channel_id=1, replica_groups=mesh['fsdp'=16,'seq'=2] {'seq'}, dimensions={1}, use_global_device_ids=true | all-gather | bytes 589824 | tf_op jit(solution)/shard_map/all_gather | solution.py:378
  253.4 3.4 all-to-all-start.8
  256.9 12.6 %all-gather.2 = bf16[256,768]{1,0:T(8,128)(2,1)S(1)} all-gather(bf16[128,768]{1,0:T(8,128)(2,1)} %copy-done.35), channel_id=4, replica_groups=mesh['fsdp'=16,'seq'=2] {'seq'}, dimensions={0}, use_global_device_ids=true | all-gather | bytes 589824 | tf_op jit(solution)/shard_map/all_gather | solution.py:379
  283.5 12.0 %all_gather.56 = bf16[1,256,768]{2,1,0:T(8,128)(2,1)S(1)} all-gather(bf16[1,128,768]{2,1,0:T(8,128)(2,1)S(1)} %multiply_convert_fusion.2), channel_id=1, replica_groups=mesh['fsdp'=16,'seq'=2] {'seq'}, dimensions={1}, use_global_device_ids=true | all-gather | bytes 589824 | tf_op jit(solution)/shard_map/all_gather | solution.py:374
  300.0 4.1 all-to-all-start.9
  304.1 8.6 %all_gather.57 = bf16[1,256,768]{1,2,0:T(8,128)(2,1)} all-gather(bf16[1,128,768]{1,2,0:T(8,128)(2,1)S(1)} %bitcast.334), channel_id=1, replica_groups=mesh['fsdp'=16,'seq'=2] {'seq'}, dimensions={1}, use_global_device_ids=true | all-gather | bytes 589824 | tf_op jit(solution)/shard_map/all_gather | solution.py:375
  325.3 3.4 all-to-all-start.10
  328.8 7.5 %all-gather = bf16[256,768]{1,0:T(8,128)(2,1)S(1)} all-gather(bf16[128,768]{1,0:T(8,128)(2,1)} %copy-done.34), channel_id=2, replica_groups=mesh['fsdp'=16,'seq'=2] {'seq'}, dimensions={0}, use_global_device_ids=true | all-gather | bytes 589824 | tf_op jit(solution)/shard_map/all_gather | solution.py:376
  347.8 6.3 %all_gather.67 = bf16[1,256,768]{2,1,0:T(8,128)(2,1)S(1)} all-gather(bf16[1,128,768]{2,1,0:T(8,128)(2,1)S(1)} %convert_element_type.326), channel_id=1, replica_groups=mesh['fsdp'=16,'seq'=2] {'seq'}, dimensions={1}, use_global_device_ids=true | all-gather | bytes 589824 | tf_op jit(solution)/shard_map/all_gather | solution.py:382
  354.1 6.5 %all-gather.4 = bf16[256,768]{1,0:T(8,128)(2,1)S(1)} all-gather(bf16[128,768]{1,0:T(8,128)(2,1)S(1)} %copy-done.13), channel_id=6, replica_groups=mesh['fsdp'=16,'seq'=2] {'seq'}, dimensions={0}, use_global_device_ids=true | all-gather | bytes 589824 | tf_op jit(solution)/shard_map/all_gather | solution.py:381
  360.6 3.6 fusion.95
  364.2 3.7 fusion.93
  367.9 3.7 fusion.88
  371.7 8.1 %pad_maximum_fusion = f32[6144,384]{1,0:T(8,128)} fusion(f32[2048,384]{1,0:T(8,128)} %fusion.88, f32[2048,384]{1,0:T(8,128)} %fusion.95, f32[2048,384]{1,0:T(8,128)} %fusion.93), kind=kLoop, calls=%fused_computation | loop fusion | flops 4718592 | bytes 18874368 | tf_op jit(solution)/shard_map/concatenate | solution.py:415
  383.8 3.3 all-to-all-start.14
  391.7 3.3 all-to-all-start.15
  395.1 3.5 fusion.20
  401.7 3.4 all-to-all-start.11
  410.1 4.3 all-to-all-start.12
  420.9 4.6 reshape.742
  425.5 4.6 pad.21
  430.1 4.8 reshape.743
  441.2 3.4 all-to-all-start.13
  458.2 3.4 all-to-all-start.17
  461.7 42.0 %all-reduce.2 = (f32[3,768]{1,0:T(4,128)}, f32[12,32]{1,0:T(8,128)}) all-reduce(f32[3,768]{1,0:T(4,128)S(1)} %pad_maximum_fusion.4, f32[12,32]{1,0:T(8,128)S(1)} %dynamic_update_slice.3), channel_id=1, replica_groups=mesh['fsdp'=16,'seq'=2] {'fsdp','seq'}, use_global_device_ids=true, to_apply=%region_13.14 | all-reduce | flops 2688 | bytes 21504 | tf_op jit(solution)/shard_map/psum | solution.py:355
  505.4 3.9 all-to-all-start.16
  510.1 58.7 %reduce-scatter.8.cloned.1.call-done = f32[384,384]{1,0:T(8,128)} async-done(((f32[6144,384]{1,0:T(8,128)}), f32[384,384]{1,0:T(8,128)}) %reduce-scatter.8.cloned.1.call-update) | async-done | bytes 589840 | tf_op jit(solution)/shard_map/reduce_scatter | solution.py:426
  570.5 3.5 all-to-all-start.18
  574.8 4.7 all-to-all-done.18
  (374 shorter events, 178.5 us)
Async XLA Ops:
  7.2 59.0 %all-gather.15.cloned.1.call-start = ((), (), s32[]{:S(2)}) async-start(), calls=%async_computation.22 | async-start | bytes 5013504 | tf_op jit(solution)/shard_map/all_gather | solution.py:201
  7.9 112.2 %all-gather.17.cloned.1.call-start = ((), (), s32[]{:S(2)}) async-start(), calls=%async_computation.23 | async-start | bytes 5013504 | tf_op jit(solution)/shard_map/all_gather | solution.py:202
  8.7 193.3 %all-gather.19.cloned.1.call-start = ((), (), s32[]{:S(2)}) async-start(), calls=%async_computation.24 | async-start | bytes 10027008 | tf_op jit(solution)/shard_map/all_gather | solution.py:207
  53.8 22.5 %copy-start.44 = (f32[768]{0:T(1024)}, f32[768]{0:T(1024)S(1)}, u32[]{:S(2)}) copy-start(f32[768]{0:T(1024)S(1)} %get-tuple-element.96) | copy-start | bytes 9220
  53.8 95.7 %copy-start.47 = (f32[768]{0:T(1024)}, f32[768]{0:T(1024)S(1)}, u32[]{:S(2)}) copy-start(f32[768]{0:T(1024)S(1)} %get-tuple-element.95) | copy-start | bytes 9220
  54.5 22.3 %copy-start.51 = (f32[128]{0:T(128)}, f32[128]{0:T(128)S(1)}, u32[]{:S(2)}) copy-start(f32[128]{0:T(128)S(1)} %get-tuple-element.107) | copy-start | bytes 1540
  71.3 8.6 %all-to-all-start = ((bf16[2,2,24576]{2,1,0:T(2,128)(2,1)}), bf16[2,2,24576]{2,1,0:T(2,128)(2,1)S(1)}, u32[]{:S(2)}, u32[]{:S(2)}) async-start(bf16[2,2,24576]{2,1,0:T(2,128)(2,1)} %reshape.797), calls=%async_computation | async-start | bytes 393216 | tf_op jit(solution)/shard_map/all_to_all | solution.py:219
  76.4 43.8 %copy-start.40 = (bf16[1,32,768]{2,1,0:T(8,128)(2,1)S(1)}, bf16[1,32,768]{2,1,0:T(8,128)(2,1)}, u32[]{:S(2)}) copy-start(bf16[1,32,768]{2,1,0:T(8,128)(2,1)} %param.27) | copy-start | bytes 147460
  79.9 8.4 %all-to-all-start.1 = ((bf16[2,2,24576]{2,1,0:T(2,128)(2,1)}), bf16[2,2,24576]{2,1,0:T(2,128)(2,1)S(1)}, u32[]{:S(2)}, u32[]{:S(2)}) async-start(bf16[2,2,24576]{2,1,0:T(2,128)(2,1)} %reshape.799), calls=%async_computation.1 | async-start | bytes 393216 | tf_op jit(solution)/shard_map/all_to_all | solution.py:217
  88.3 39.1 %all-to-all-start.2 = ((bf16[2,2,24576]{2,1,0:T(2,128)(2,1)}), bf16[2,2,24576]{2,1,0:T(2,128)(2,1)S(1)}, u32[]{:S(2)}, u32[]{:S(2)}) async-start(bf16[2,2,24576]{2,1,0:T(2,128)(2,1)} %reshape.801), calls=%async_computation.2 | async-start | bytes 393216 | tf_op jit(solution)/shard_map/all_to_all | solution.py:218
  131.8 15.2 %copy-start.23 = (bf16[6,64,256]{2,1,0:T(8,128)(2,1)}, bf16[6,64,256]{2,1,0:T(8,128)(2,1)S(1)}, u32[]{:S(2)}) copy-start(bf16[6,64,256]{2,1,0:T(8,128)(2,1)S(1)} %convolution_convert_fusion.11) | copy-start | bytes 589828
  134.8 8.6 %all-to-all-start.3 = ((bf16[2,2,24576]{2,1,0:T(2,128)(2,1)}), bf16[2,2,24576]{2,1,0:T(2,128)(2,1)S(1)}, u32[]{:S(2)}, u32[]{:S(2)}) async-start(bf16[2,2,24576]{2,1,0:T(2,128)(2,1)} %reshape.803), calls=%async_computation.3 | async-start | bytes 393216 | tf_op jit(solution)/shard_map/all_to_all | solution.py:228
  143.4 7.3 %all-to-all-start.4 = ((bf16[2,2,6144]{2,1,0:T(2,128)(2,1)}), bf16[2,2,6144]{2,1,0:T(2,128)(2,1)S(1)}, u32[]{:S(2)}, u32[]{:S(2)}) async-start(bf16[2,2,6144]{2,1,0:T(2,128)(2,1)} %reshape.805), calls=%async_computation.4 | async-start | bytes 98304 | tf_op jit(solution)/shard_map/all_to_all | solution.py:248
  147.1 11.4 %copy-start.16 = (bf16[1,128,2,384]{1,3,2,0:T(8,128)(2,1)}, bf16[1,128,2,384]{1,3,2,0:T(8,128)(2,1)S(1)}, u32[]{:S(2)}) copy-start(bf16[1,128,2,384]{1,3,2,0:T(8,128)(2,1)S(1)} %copy.223) | copy-start | bytes 589828
  150.7 7.9 %all-to-all-start.6 = ((bf16[2,2,6144]{2,1,0:T(2,128)(2,1)}), bf16[2,2,6144]{2,1,0:T(2,128)(2,1)S(1)}, u32[]{:S(2)}, u32[]{:S(2)}) async-start(bf16[2,2,6144]{2,1,0:T(2,128)(2,1)} %reshape.807), calls=%async_computation.6 | async-start | bytes 98304 | tf_op jit(solution)/shard_map/all_to_all | solution.py:247
  158.6 8.2 %all-to-all-start.5 = ((bf16[2,2,24576]{2,1,0:T(2,128)(2,1)}), bf16[2,2,24576]{2,1,0:T(2,128)(2,1)S(1)}, u32[]{:S(2)}, u32[]{:S(2)}) async-start(bf16[2,2,24576]{2,1,0:T(2,128)(2,1)} %reshape.809), calls=%async_computation.5 | async-start | bytes 393216 | tf_op jit(solution)/shard_map/all_to_all | solution.py:246
  162.0 198.6 %all-gather.23.cloned.1.call-start = ((), (), s32[]{:S(2)}) async-start(), calls=%async_computation.29 | async-start | bytes 1572864 | tf_op jit(solution)/shard_map/all_gather | solution.py:384
  168.1 17.1 %copy-start.20 = (bf16[6,64,256]{2,1,0:T(8,128)(2,1)}, bf16[6,64,256]{2,1,0:T(8,128)(2,1)S(1)}, u32[]{:S(2)}) copy-start(bf16[6,64,256]{2,1,0:T(8,128)(2,1)S(1)} %convolution_convert_fusion.3) | copy-start | bytes 589828
  168.1 33.8 %copy-start.7 = (f32[1,128,768]{2,1,0:T(8,128)S(1)}, f32[1,128,768]{2,1,0:T(8,128)}, u32[]{:S(2)}) copy-start(f32[1,128,768]{2,1,0:T(8,128)} %param.35) | copy-start | bytes 1179652
  187.1 59.8 %copy-start.9 = (f32[128,768]{1,0:T(8,128)}, f32[128,768]{1,0:T(8,128)S(1)}, u32[]{:S(2)}) copy-start(f32[128,768]{1,0:T(8,128)S(1)} %get-tuple-element.119) | copy-start | bytes 1179652
  212.7 151.5 %all-gather.21.cloned.1.call-start = ((), (), s32[]{:S(2)}) async-start(), calls=%async_computation.28 | async-start | bytes 1572864 | tf_op jit(solution)/shard_map/all_gather | solution.py:383
  250.8 23.6 %copy-start.21 = (bf16[6,64,256]{2,1,0:T(8,128)(2,1)S(1)}, bf16[6,64,256]{2,1,0:T(8,128)(2,1)}, u32[]{:S(2)}) copy-start(bf16[6,64,256]{2,1,0:T(8,128)(2,1)} %copy-done.20) | copy-start | bytes 589828
  253.4 18.7 %all-to-all-start.8 = ((bf16[2,2,24576]{2,1,0:T(2,128)(2,1)}), bf16[2,2,24576]{2,1,0:T(2,128)(2,1)S(1)}, u32[]{:S(2)}, u32[]{:S(2)}) async-start(bf16[2,2,24576]{2,1,0:T(2,128)(2,1)} %reshape.813), calls=%async_computation.8 | async-start | bytes 393216 | tf_op jit(solution)/shard_map/all_to_all | solution.py:281
  256.9 111.1 %all-gather.25.cloned.1.call-start = ((), (), s32[]{:S(2)}) async-start(), calls=%async_computation.30 | async-start | bytes 1572864 | tf_op jit(solution)/shard_map/all_gather | solution.py:385
  269.5 187.1 %reduce-scatter.6.cloned.1.call-start = ((), (), s32[]{:S(2)}) async-start(), calls=%async_computation.26 | async-start | bytes 5013504 | tf_op jit(solution)/shard_map/reduce_scatter | solution.py:425
  282.7 21.4 %copy-start.17 = (bf16[1,128,2,384]{1,3,2,0:T(8,128)(2,1)S(1)}, bf16[1,128,2,384]{1,3,2,0:T(8,128)(2,1)}, u32[]{:S(2)}) copy-start(bf16[1,128,2,384]{1,3,2,0:T(8,128)(2,1)} %copy-done.16) | copy-start | bytes 589828
  283.4 32.3 %copy-start.48 = (f32[768]{0:T(1024)S(1)}, f32[768]{0:T(1024)}, u32[]{:S(2)}) copy-start(f32[768]{0:T(1024)} %copy-done.47) | copy-start | bytes 9220
  295.5 44.4 %copy-start.3 = (bf16[1,256,768]{2,1,0:T(8,128)(2,1)}, bf16[1,256,768]{2,1,0:T(8,128)(2,1)S(1)}, u32[]{:S(2)}) copy-start(bf16[1,256,768]{2,1,0:T(8,128)(2,1)S(1)} %all_gather.56) | copy-start | bytes 1179652
  295.5 22.7 %copy-start.25 = (f32[128,768]{1,0:T(8,128)S(1)}, f32[128,768]{1,0:T(8,128)}, u32[]{:S(2)}) copy-start(f32[128,768]{1,0:T(8,128)} %get-tuple-element.102) | copy-start | bytes 1179652
  300.0 12.6 %all-to-all-start.9 = ((bf16[2,2,24576]{2,1,0:T(2,128)(2,1)}), bf16[2,2,24576]{2,1,0:T(2,128)(2,1)}, u32[]{:S(2)}, u32[]{:S(2)}) async-start(bf16[2,2,24576]{2,1,0:T(2,128)(2,1)} %reshape.815), calls=%async_computation.9 | async-start | bytes 393216 | tf_op jit(solution)/shard_map/all_to_all | solution.py:300
  322.4 17.0 %copy-start.24 = (bf16[6,64,256]{2,1,0:T(8,128)(2,1)S(1)}, bf16[6,64,256]{2,1,0:T(8,128)(2,1)}, u32[]{:S(2)}) copy-start(bf16[6,64,256]{2,1,0:T(8,128)(2,1)} %copy-done.23) | copy-start | bytes 589828
  325.3 13.5 %all-to-all-start.10 = ((bf16[2,2,24576]{2,1,0:T(2,128)(2,1)}), bf16[2,2,24576]{2,1,0:T(2,128)(2,1)S(1)}, u32[]{:S(2)}, u32[]{:S(2)}) async-start(bf16[2,2,24576]{2,1,0:T(2,128)(2,1)} %reshape.817), calls=%async_computation.10 | async-start | bytes 393216 | tf_op jit(solution)/shard_map/all_to_all | solution.py:315
  328.8 174.9 %reduce-scatter.4.cloned.1.call-start = ((), (), s32[]{:S(2)}) async-start(), calls=%async_computation.25 | async-start | bytes 5013504 | tf_op jit(solution)/shard_map/reduce_scatter | solution.py:424
  346.8 222.0 %reduce-scatter.8.cloned.1.call-start = ((), (), s32[]{:S(2)}) async-start(), calls=%async_computation.27 | async-start | bytes 10027008 | tf_op jit(solution)/shard_map/reduce_scatter | solution.py:426
  379.7 15.3 %copy-start.10 = (f32[128,768]{1,0:T(8,128)S(1)}, f32[128,768]{1,0:T(8,128)}, u32[]{:S(2)}) copy-start(f32[128,768]{1,0:T(8,128)} %copy-done.9) | copy-start | bytes 1179652
  379.7 15.3 %copy-start.38 = (bf16[128,2048]{1,0:T(8,128)(2,1)S(1)}, bf16[128,2048]{1,0:T(8,128)(2,1)}, u32[]{:S(2)}) copy-start(bf16[128,2048]{1,0:T(8,128)(2,1)} %get-tuple-element.105) | copy-start | bytes 1572868
  379.8 18.8 %copy-start.54 = (f32[768]{0:T(1024)S(1)}, f32[768]{0:T(1024)}, u32[]{:S(2)}) copy-start(f32[768]{0:T(1024)} %get-tuple-element.92) | copy-start | bytes 9220
  383.8 7.3 %all-to-all-start.14 = ((bf16[2,2,6144]{2,1,0:T(2,128)(2,1)}), bf16[2,2,6144]{2,1,0:T(2,128)(2,1)S(1)}, u32[]{:S(2)}, u32[]{:S(2)}) async-start(bf16[2,2,6144]{2,1,0:T(2,128)(2,1)} %reshape.825), calls=%async_computation.14 | async-start | bytes 98304 | tf_op jit(solution)/shard_map/all_to_all | solution.py:301
  391.7 10.0 %all-to-all-start.15 = ((bf16[2,2,6144]{2,1,0:T(2,128)(2,1)}), bf16[2,2,6144]{2,1,0:T(2,128)(2,1)S(1)}, u32[]{:S(2)}, u32[]{:S(2)}) async-start(bf16[2,2,6144]{2,1,0:T(2,128)(2,1)} %reshape.827), calls=%async_computation.15 | async-start | bytes 98304 | tf_op jit(solution)/shard_map/all_to_all | solution.py:302
  401.0 15.9 %copy-start.55 = (f32[768]{0:T(1024)S(1)}, f32[768]{0:T(1024)}, u32[]{:S(2)}) copy-start(f32[768]{0:T(1024)} %get-tuple-element.90) | copy-start | bytes 9220
  401.7 8.4 %all-to-all-start.11 = ((bf16[2,2,24576]{2,1,0:T(2,128)(2,1)}), bf16[2,2,24576]{2,1,0:T(2,128)(2,1)S(1)}, u32[]{:S(2)}, u32[]{:S(2)}) async-start(bf16[2,2,24576]{2,1,0:T(2,128)(2,1)} %reshape.819), calls=%async_computation.11 | async-start | bytes 393216 | tf_op jit(solution)/shard_map/all_to_all | solution.py:334
  410.1 31.2 %all-to-all-start.12 = ((bf16[2,2,24576]{2,1,0:T(2,128)(2,1)}), bf16[2,2,24576]{2,1,0:T(2,128)(2,1)}, u32[]{:S(2)}, u32[]{:S(2)}) async-start(bf16[2,2,24576]{2,1,0:T(2,128)(2,1)} %reshape.821), calls=%async_computation.12 | async-start | bytes 393216 | tf_op jit(solution)/shard_map/all_to_all | solution.py:335
  441.2 8.3 %all-to-all-start.13 = ((bf16[2,2,24576]{2,1,0:T(2,128)(2,1)}), bf16[2,2,24576]{2,1,0:T(2,128)(2,1)S(1)}, u32[]{:S(2)}, u32[]{:S(2)}) async-start(bf16[2,2,24576]{2,1,0:T(2,128)(2,1)} %reshape.823), calls=%async_computation.13 | async-start | bytes 393216 | tf_op jit(solution)/shard_map/all_to_all | solution.py:336
  451.8 9.8 %copy-start.50 = (f32[1,768]{1,0:T(1,128)S(1)}, f32[1,768]{1,0:T(1,128)}, u32[]{:S(2)}) copy-start(f32[1,768]{1,0:T(1,128)} %stack.13) | copy-start | bytes 9220
  458.2 47.1 %all-to-all-start.17 = ((bf16[2,96,384]{2,1,0:T(8,128)(2,1)}), bf16[2,96,384]{2,1,0:T(8,128)(2,1)S(1)}, u32[]{:S(2)}, u32[]{:S(2)}) async-start(bf16[2,96,384]{2,1,0:T(8,128)(2,1)} %bitcast.97), calls=%async_computation.19 | async-start | bytes 294912 | tf_op jit(solution)/shard_map/all_to_all | solution.py:432
  461.7 118.7 %copy-start.1 = (f32[12,32]{1,0:T(8,128)S(1)}, f32[12,32]{1,0:T(8,128)}, u32[]{:S(2)}) copy-start(f32[12,32]{1,0:T(8,128)} %param.32) | copy-start | bytes 4612
  505.4 65.2 %all-to-all-start.16 = ((bf16[2,96,384]{2,1,0:T(8,128)(2,1)}), bf16[2,96,384]{2,1,0:T(8,128)(2,1)S(1)}, u32[]{:S(2)}, u32[]{:S(2)}) async-start(bf16[2,96,384]{2,1,0:T(8,128)(2,1)} %bitcast.84), calls=%async_computation.17 | async-start | bytes 294912 | tf_op jit(solution)/shard_map/all_to_all | solution.py:429
  570.5 8.9 %all-to-all-start.18 = ((bf16[2,192,384]{2,1,0:T(8,128)(2,1)}), bf16[2,192,384]{2,1,0:T(8,128)(2,1)S(1)}, u32[]{:S(2)}, u32[]{:S(2)}) async-start(bf16[2,192,384]{2,1,0:T(8,128)(2,1)} %bitcast.100), calls=%async_computation.21 | async-start | bytes 589824 | tf_op jit(solution)/shard_map/all_to_all | solution.py:435
  (41 other events, 138.5 us)
Sparse Core Ops, SparseCore 0:
  10.3 55.8 all-gather.14
  68.4 51.6 all-gather.16
  122.4 79.4 all-gather.18
  212.9 24.4 all-gather.22
  241.1 26.0 all-gather.20
  269.6 26.2 all-gather.24
  299.7 75.5 reduce-scatter.5
  379.2 74.8 reduce-scatter.3
  458.2 110.5 reduce-scatter.7
where the time goes:
time: 599 us; the launch traced here: 587 us
  blocking collectives  155 us (26%)
  waiting for transfers between devices  125 us (21%)
  local copies, waits for them, and re-layouts  88.1 us (15%)
  matrix products  80.1 us (13%)
  starting transfers between devices  64.4 us (11%)
  other arithmetic  58 us (10%)
  between operations  15.9 us (3%)
    reduce_scatter x1, waiting for transfers between devices, local(): lax.psum_scatter(feed_slab, 'fsdp', scatter_dimension=0, tiled=True)  58.7 us
    psum x1, blocking collectives, local(): lax.psum((gain_grads, table_full), ('fsdp', 'seq'))  42 us
    unnamed x179, local copies, waits for them, and re-layouts  33.3 us
    unnamed x19, other arithmetic  30.7 us
    all_gather x1, waiting for transfers between devices, attn_gather(): lax.all_gather(cross_weights, 'fsdp', axis=0, tiled=True)  28.4 us
    dot_general x11, matrix products, contract_cols(): lax.dot_general(left, right, (((1,), (1,)), ((), ())), preferred_element_...  26.9 us
    all_gather x1, blocking collectives, attn_gather(): lax.all_gather(norm_gains, 'fsdp', axis=1, tiled=True)  23.5 us
    dot_general x11, matrix products, contract_rows(): lax.dot_general(left, right, (((0,), (0,)), ((), ())), preferred_element_...  20 us
  transfers between devices with their start and end apart: 27, of which 12 were waited for; matrix products, arithmetic and copies ran while one was open for 35% of the time, Pallas kernels for 0%

commit v1 on v0

v1 whole, which is shorter than its diff:
```python
import functools
import math

import jax
import jax.numpy as jnp
import numpy as np
from jax import lax
from jax.experimental import pallas as pl
from jax.experimental.pallas import tpu as pltpu
from jax.sharding import PartitionSpec as P

H = 12
DK = 64
F = 2048
EPS = 1e-06
GELU_SCALE = math.sqrt(2.0 / math.pi)
BF = jnp.bfloat16
F32 = jnp.float32
VMEM_SPEC = pl.BlockSpec(memory_space=pltpu.VMEM)
SMEM_SPEC = pl.BlockSpec(memory_space=pltpu.SMEM)
PARAMS = pltpu.CompilerParams(vmem_limit_bytes=56 * 1024 * 1024)


def dot_nn(a, b):
    return lax.dot_general(a, b, (((1,), (0,)), ((), ())), preferred_element_type=F32)


def dot_nt(a, b):
    return lax.dot_general(a, b, (((1,), (1,)), ((), ())), preferred_element_type=F32)


def dot_tn(a, b):
    return lax.dot_general(a, b, (((0,), (0,)), ((), ())), preferred_element_type=F32)


def rms_scale(rows):
    return lax.rsqrt(jnp.mean(rows * rows, axis=-1, keepdims=True) + EPS)


def norm_back(rows, gain, dnorm):
    scale = rms_scale(rows)
    gained = gain * dnorm
    inner = jnp.mean(rows * gained, axis=-1, keepdims=True)
    drows = scale * gained - rows * (scale * scale * scale) * inner
    dgain = jnp.sum(dnorm * rows * scale, axis=0, keepdims=True)
    return drows, dgain


def half_masks():
    lane = lax.broadcasted_iota(jnp.int32, (1, 2 * DK), 1)
    low = jnp.where(lane < DK, 1.0, 0.0)
    return low.astype(F32), (1.0 - low).astype(F32)


def softmax_rows(scores):
    row_max = jnp.max(scores, axis=-1, keepdims=True)
    expd = jnp.exp(scores - row_max)
    return expd / jnp.sum(expd, axis=-1, keepdims=True)


def qkv_kernel(stream_ref, gain_ref, w_ref, q_ref, kv_ref, n1t_ref, norm_ref):
    step = pl.program_id(0)

    @pl.when(step == 0)
    def _():
        rows = stream_ref[...]
        normed = rows * rms_scale(rows) * gain_ref[0:1]
        norm_ref[...] = normed.astype(BF)
        n1t_ref[...] = normed.T.astype(BF)

    out = dot_nn(norm_ref[...], w_ref[...]).astype(BF)

    @pl.when(step == 0)
    def _():
        q_ref[...] = out

    @pl.when(step > 0)
    def _():
        kv_ref[0] = out


def run_qkv(stream, gains, self_full):
    tokens, features = stream.shape
    return pl.pallas_call(
        qkv_kernel,
        grid=(3,),
        in_specs=[
            pl.BlockSpec((tokens, features), lambda i: (0, 0)),
            pl.BlockSpec((3, features), lambda i: (0, 0)),
            pl.BlockSpec((features, features), lambda i: (i, 0)),
        ],
        out_specs=[
            pl.BlockSpec((tokens, features), lambda i: (0, 0)),
            pl.BlockSpec((1, tokens, features), lambda i: (jnp.maximum(i - 1, 0), 0, 0)),
            pl.BlockSpec((features, tokens), lambda i: (0, 0)),
        ],
        out_shape=[
            jax.ShapeDtypeStruct((tokens, features), BF),
            jax.ShapeDtypeStruct((2, tokens, features), BF),
            jax.ShapeDtypeStruct((features, tokens), BF),
        ],
        scratch_shapes=[pltpu.VMEM((tokens, features), BF)],
        compiler_params=PARAMS,
        name="qkv",
    )(stream, gains, self_full)


def join_pieces(own, others, which):
    return jnp.concatenate([own[which]] + [piece[which] for piece in others], axis=0)


def self_fwd_kernel(group_size, *refs):
    pos_ref, q_ref, kv_ref = refs[:3]
    other_refs = refs[3 : 2 + group_size]
    keep_ref, bias_ref, stream_ref, w_ref, gain_ref = refs[2 + group_size : 7 + group_size]
    prob_ref, ctx_ref, ctxt_ref, after_ref, n2_ref, n2t_ref = refs[7 + group_size :]
    tokens = q_ref.shape[0]
    total = tokens * group_size
    pos = pos_ref[0]
    keys = join_pieces(kv_ref, other_refs, 0)
    values = join_pieces(kv_ref, other_refs, 1)
    row = lax.broadcasted_iota(jnp.int32, (tokens, total), 0)
    col = lax.broadcasted_iota(jnp.int32, (tokens, total), 1)
    keep = jnp.broadcast_to(keep_ref[...], (tokens, total)) > 0
    earlier = (col >= tokens) & (pos * tokens + col >= total)
    allowed = (col == row) | (keep & ((col < row) | earlier))
    masks = half_masks()
    lane_low = lax.broadcasted_iota(jnp.int32, (tokens, 2 * DK), 1) < DK
    for pair in range(H // 2):
        cols = slice(pair * 2 * DK, (pair + 1) * 2 * DK)
        query_pair = q_ref[:, cols]
        key_pair = keys[:, cols]
        value_pair = values[:, cols]
        parts = []
        for half in range(2):
            head = pair * 2 + half
            scores = dot_nt(query_pair * masks[half].astype(BF), key_pair)
            line = jnp.broadcast_to(bias_ref[head : head + 1, :], (tokens, total))
            scores = scores + pltpu.roll(line, 0, 1, stride=1, stride_axis=0)
            prob = softmax_rows(jnp.where(allowed, scores, -jnp.inf))
            prob_ref[head] = prob
            parts.append(dot_nn(prob.astype(BF), value_pair))
        ctx_pair = jnp.where(lane_low, parts[0], parts[1])
        ctx_ref[:, cols] = ctx_pair.astype(BF)
        ctxt_ref[cols, :] = ctx_pair.T.astype(BF)
    after = stream_ref[...] + dot_nn(ctx_ref[...], w_ref[...])
    after_ref[...] = after
    normed = after * rms_scale(after) * gain_ref[1:2]
    n2_ref[...] = normed.astype(BF)
    n2t_ref[...] = normed.T.astype(BF)


def run_self_fwd(pos, q, kv, others, keep, bias_line, stream, self_full, gains):
    tokens, features = stream.shape
    group_size = len(others) + 1
    total = tokens * group_size
    return pl.pallas_call(
        functools.partial(self_fwd_kernel, group_size),
        grid=(1,),
        in_specs=[SMEM_SPEC, VMEM_SPEC, VMEM_SPEC]
        + [VMEM_SPEC] * len(others)
        + [VMEM_SPEC, VMEM_SPEC, VMEM_SPEC]
        + [pl.BlockSpec((features, features), lambda i: (3, 0)), VMEM_SPEC],
        out_specs=[VMEM_SPEC] * 6,
        out_shape=[
            jax.ShapeDtypeStruct((H, tokens, total), F32),
            jax.ShapeDtypeStruct((tokens, features), BF),
            jax.ShapeDtypeStruct((features, tokens), BF),
            jax.ShapeDtypeStruct((tokens, features), F32),
            jax.ShapeDtypeStruct((tokens, features), BF),
            jax.ShapeDtypeStruct((features, tokens), BF),
        ],
        compiler_params=PARAMS,
        name="self_fwd",
    )(pos, q, kv, *others, keep, bias_line, stream, self_full, gains)


def cross_fwd_kernel(
    after_ref, n2_ref, enc_ref, w_ref, gain_ref,
    prob_ref, cq_ref, ckv_ref, ctx_ref, ctxt_ref, out_ref, n3_ref,
):
    tokens, features = n2_ref.shape
    cq_ref[...] = dot_nn(n2_ref[...], w_ref[0:features]).astype(BF)
    ckv_ref[0] = dot_nn(enc_ref[...], w_ref[features : 2 * features]).astype(BF)
    ckv_ref[1] = dot_nn(enc_ref[...], w_ref[2 * features : 3 * features]).astype(BF)
    masks = half_masks()
    lane_low = lax.broadcasted_iota(jnp.int32, (tokens, 2 * DK), 1) < DK
    for pair in range(H // 2):
        cols = slice(pair * 2 * DK, (pair + 1) * 2 * DK)
        query_pair = cq_ref[:, cols]
        key_pair = ckv_ref[0, :, cols]
        value_pair = ckv_ref[1, :, cols]
        parts = []
        for half in range(2):
            scores = dot_nt(query_pair * masks[half].astype(BF), key_pair)
            prob = softmax_rows(scores)
            prob_ref[pair * 2 + half] = prob
            parts.append(dot_nn(prob.astype(BF), value_pair))
        ctx_pair = jnp.where(lane_low, parts[0], parts[1])
        ctx_ref[:, cols] = ctx_pair.astype(BF)
        ctxt_ref[cols, :] = ctx_pair.T.astype(BF)
    after = after_ref[...] + dot_nn(ctx_ref[...], w_ref[3 * features : 4 * features])
    out_ref[...] = after
    n3_ref[...] = (after * rms_scale(after) * gain_ref[2:3]).astype(BF)


def run_cross_fwd(after_self, n2, enc_all, cross_full, gains):
    tokens, features = after_self.shape
    enc_len = enc_all.shape[0]
    return pl.pallas_call(
        cross_fwd_kernel,
        in_specs=[VMEM_SPEC] * 5,
        out_specs=[VMEM_SPEC] * 7,
        out_shape=[
            jax.ShapeDtypeStruct((H, tokens, enc_len), F32),
            jax.ShapeDtypeStruct((tokens, features), BF),
            jax.ShapeDtypeStruct((2, enc_len, features), BF),
            jax.ShapeDtypeStruct((tokens, features), BF),
            jax.ShapeDtypeStruct((features, tokens), BF),
            jax.ShapeDtypeStruct((tokens, features), F32),
            jax.ShapeDtypeStruct((tokens, features), BF),
        ],
        compiler_params=PARAMS,
        name="cross_fwd",
    )(after_self, n2, enc_all, cross_full, gains)


def gelu_parts(value):
    tangent = jnp.tanh(GELU_SCALE * (value + 0.044715 * value * value * value))
    result = 0.5 * value * (1.0 + tangent)
    slope = 0.5 * (1.0 + tangent) + 0.5 * value * (1.0 - tangent * tangent) * GELU_SCALE * (
        1.0 + 3.0 * 0.044715 * value * value
    )
    return result, slope


def feed_kernel(
    n3_ref, grad_ref, after_ref, gain_ref, g0_ref, g1_ref, g2_ref,
    hgu_ref, out_ref, in_grad_ref, dgain_ref, cot_ref, acc_ref,
):
    step = pl.program_id(0)
    last = pl.num_programs(0) - 1

    @pl.when(step == 0)
    def _():
        cot_ref[...] = grad_ref[...].astype(BF)
        out_ref[...] = after_ref[...]
        acc_ref[...] = jnp.zeros_like(acc_ref)

    n3 = n3_ref[...]
    gate_pre = dot_nt(g0_ref[...], n3)
    up_pre = dot_nt(g1_ref[...], n3)
    hidden_grad = dot_nt(g2_ref[...], cot_ref[...])
    gate_act, gate_slope = gelu_parts(gate_pre)
    hidden = (gate_act * up_pre).astype(BF)
    gate_grad = (hidden_grad * up_pre * gate_slope).astype(BF)
    up_grad = (hidden_grad * gate_act).astype(BF)
    hgu_ref[0] = gate_grad
    hgu_ref[1] = up_grad
    hgu_ref[2] = hidden
    out_ref[...] += dot_tn(hidden, g2_ref[...])
    acc_ref[...] += dot_tn(gate_grad, g0_ref[...]) + dot_tn(up_grad, g1_ref[...])

    @pl.when(step == last)
    def _():
        drows, dgain = norm_back(after_ref[...], gain_ref[2:3], acc_ref[...])
        in_grad_ref[...] = grad_ref[...] + drows
        dgain_ref[...] = dgain


def run_feed(n3, out_grad, after_cross, gains, feed_full):
    tokens, features = out_grad.shape
    block = 256
    steps = F // block
    whole = pl.BlockSpec((tokens, features), lambda i: (0, 0))
    return pl.pallas_call(
        feed_kernel,
        grid=(steps,),
        in_specs=[
            whole,
            whole,
            whole,
            pl.BlockSpec((3, features), lambda i: (0, 0)),
            pl.BlockSpec((block, features), lambda i: (i, 0)),
            pl.BlockSpec((block, features), lambda i: (i + steps, 0)),
            pl.BlockSpec((block, features), lambda i: (i + 2 * steps, 0)),
        ],
        out_specs=[
            pl.BlockSpec((3, block, tokens), lambda i: (0, i, 0)),
            whole,
            whole,
            pl.BlockSpec((1, features), lambda i: (0, 0)),
        ],
        out_shape=[
            jax.ShapeDtypeStruct((3, F, tokens), BF),
            jax.ShapeDtypeStruct((tokens, features), F32),
            jax.ShapeDtypeStruct((tokens, features), F32),
            jax.ShapeDtypeStruct((1, features), F32),
        ],
        scratch_shapes=[pltpu.VMEM((tokens, features), BF), pltpu.VMEM((tokens, features), F32)],
        compiler_params=PARAMS,
        name="feed",
    )(n3, out_grad, after_cross, gains, feed_full, feed_full, feed_full)


def cross_bwd_kernel(
    in_grad_ref, w_ref, prob_ref, ctx_ref, cq_ref, ckv_ref, after_ref, gain_ref,
    pack_ref, enc_pack_ref, out_ref, dgain_ref,
):
    tokens, features = cq_ref.shape
    low = in_grad_ref[...].astype(BF)
    pack_ref[0] = low
    ctx_grad = dot_nt(low, w_ref[3 * features : 4 * features]).astype(BF)
    masks = half_masks()
    lane_low = lax.broadcasted_iota(jnp.int32, (tokens, 2 * DK), 1) < DK
    enc_low = lax.broadcasted_iota(jnp.int32, (ckv_ref.shape[1], 2 * DK), 1) < DK
    for pair in range(H // 2):
        cols = slice(pair * 2 * DK, (pair + 1) * 2 * DK)
        grad_pair = ctx_grad[:, cols]
        query_pair = cq_ref[:, cols]
        key_pair = ckv_ref[0, :, cols]
        value_pair = ckv_ref[1, :, cols]
        weighted = ctx_ref[:, cols].astype(F32) * grad_pair.astype(F32)
        dq, dk, dv = [], [], []
        for half in range(2):
            prob = prob_ref[pair * 2 + half]
            delta = jnp.sum(weighted * masks[half], axis=-1, keepdims=True)
            prob_grad = dot_nt(grad_pair * masks[half].astype(BF), value_pair)
            score_low = (prob * (prob_grad - delta)).astype(BF)
            dq.append(dot_nn(score_low, key_pair))
            dk.append(dot_tn(score_low, query_pair))
            dv.append(dot_tn(prob.astype(BF), grad_pair))
        pack_ref[1, :, cols] = jnp.where(lane_low, dq[0], dq[1]).astype(BF)
        enc_pack_ref[0, :, cols] = jnp.where(enc_low, dk[0], dk[1]).astype(BF)
        enc_pack_ref[1, :, cols] = jnp.where(enc_low, dv[0], dv[1]).astype(BF)
    n2_grad = dot_nt(pack_ref[1], w_ref[0:features])
    drows, dgain = norm_back(after_ref[...], gain_ref[1:2], n2_grad)
    self_in = in_grad_ref[...] + drows
    out_ref[...] = self_in
    pack_ref[2] = self_in.astype(BF)
    dgain_ref[...] = dgain


def run_cross_bwd(in_grad, cross_full, prob, ctx, cq, ckv, after_self, gains):
    tokens, features = in_grad.shape
    return pl.pallas_call(
        cross_bwd_kernel,
        in_specs=[VMEM_SPEC] * 8,
        out_specs=[VMEM_SPEC] * 4,
        out_shape=[
            jax.ShapeDtypeStruct((3, tokens, features), BF),
            jax.ShapeDtypeStruct(ckv.shape, BF),
            jax.ShapeDtypeStruct((tokens, features), F32),
            jax.ShapeDtypeStruct((1, features), F32),
        ],
        compiler_params=PARAMS,
        name="cross_bwd",
    )(in_grad, cross_full, prob, ctx, cq, ckv, after_self, gains)


def unskew(grid):
    tokens, total = grid.shape
    row = lax.broadcasted_iota(jnp.int32, (tokens, total), 0)
    step = 1
    while step < tokens:
        moved = pltpu.roll(grid, total - step, 1)
        grid = jnp.where((row & step) != 0, moved, grid)
        step *= 2
    return jnp.sum(grid, axis=0, keepdims=True)


def self_bwd_kernel(group_size, *refs):
    low_ref, w_ref, prob_ref, ctx_ref, q_ref, kv_ref = refs[:6]
    other_refs = refs[6 : 5 + group_size]
    pack_ref, dist_ref = refs[5 + group_size :]
    tokens = q_ref.shape[0]
    ctx_grad = dot_nt(low_ref[0], w_ref[...]).astype(BF)
    keys = join_pieces(kv_ref, other_refs, 0)
    values = join_pieces(kv_ref, other_refs, 1)
    masks = half_masks()
    lane_low = lax.broadcasted_iota(jnp.int32, (tokens, 2 * DK), 1) < DK
    key_low = lax.broadcasted_iota(jnp.int32, (tokens * group_size, 2 * DK), 1) < DK
    for pair in range(H // 2):
        cols = slice(pair * 2 * DK, (pair + 1) * 2 * DK)
        grad_pair = ctx_grad[:, cols]
        query_pair = q_ref[:, cols]
        key_pair = keys[:, cols]
        value_pair = values[:, cols]
        weighted = ctx_ref[:, cols].astype(F32) * grad_pair.astype(F32)
        dq, dk, dv = [], [], []
        for half in range(2):
            head = pair * 2 + half
            prob = prob_ref[head]
            delta = jnp.sum(weighted * masks[half], axis=-1, keepdims=True)
            prob_grad = dot_nt(grad_pair * masks[half].astype(BF), value_pair)
            score_grad = prob * (prob_grad - delta)
            dist_ref[head : head + 1, :] = unskew(score_grad)
            score_low = score_grad.astype(BF)
            dq.append(dot_nn(score_low, key_pair))
            dk.append(dot_tn(score_low, query_pair))
            dv.append(dot_tn(prob.astype(BF), grad_pair))
        pack_ref[0, :, cols] = jnp.where(lane_low, dq[0], dq[1]).astype(BF)
        dk_pair = jnp.where(key_low, dk[0], dk[1]).astype(BF)
        dv_pair = jnp.where(key_low, dv[0], dv[1]).astype(BF)
        for piece in range(group_size):
            rows = slice(piece * tokens, (piece + 1) * tokens)
            pack_ref[1 + piece, :, cols] = dk_pair[rows]
            pack_ref[1 + group_size + piece, :, cols] = dv_pair[rows]


def run_self_bwd(cross_pack, self_full, prob, ctx, q, kv, others):
    tokens, features = q.shape
    group_size = len(others) + 1
    return pl.pallas_call(
        functools.partial(self_bwd_kernel, group_size),
        grid=(1,),
        in_specs=[
            pl.BlockSpec((1, tokens, features), lambda i: (2, 0, 0)),
            pl.BlockSpec((features, features), lambda i: (3, 0)),
        ]
        + [VMEM_SPEC] * (3 + group_size),
        out_specs=[VMEM_SPEC] * 2,
        out_shape=[
            jax.ShapeDtypeStruct((1 + 2 * group_size, tokens, features), BF),
            jax.ShapeDtypeStruct((H, tokens * group_size), F32),
        ],
        compiler_params=PARAMS,
        name="self_bwd",
    )(cross_pack, self_full, prob, ctx, q, kv, *others)


def qkv_bwd_kernel(group_size, *refs):
    pack_refs = refs[:group_size]
    w_ref, stream_ref, gain_ref, in_grad_ref = refs[group_size : group_size + 4]
    sums_ref, out_ref, dgain_ref, acc_ref = refs[group_size + 4 :]
    step = pl.program_id(0)

    @pl.when(step == 0)
    def _():
        for source in range(group_size):
            sums_ref[0, source] = pack_refs[source][0]
        acc_ref[...] = dot_nt(pack_refs[0][0], w_ref[...])

    @pl.when(step > 0)
    def _():
        base = 1 + (step - 1) * group_size
        for piece in range(group_size):
            total = None
            for source in range(group_size):
                part = pack_refs[source][base + (piece - source) % group_size].astype(F32)
                total = part if total is None else total + part
            sums_ref[0, piece] = total.astype(BF)
        acc_ref[...] += dot_nt(sums_ref[0, 0], w_ref[...])

    @pl.when(step == 2)
    def _():
        drows, dgain = norm_back(stream_ref[...], gain_ref[0:1], acc_ref[...])
        out_ref[...] = in_grad_ref[...] + drows
        dgain_ref[...] = dgain


def run_qkv_bwd(packs, self_full, stream, gains, self_in_grad):
    tokens, features = stream.shape
    group_size = len(packs)
    whole = pl.BlockSpec((tokens, features), lambda i: (0, 0))
    pack_spec = pl.BlockSpec((1 + 2 * group_size, tokens, features), lambda i: (0, 0, 0))
    return pl.pallas_call(
        functools.partial(qkv_bwd_kernel, group_size),
        grid=(3,),
        in_specs=[pack_spec] * group_size
        + [
            pl.BlockSpec((features, features), lambda i: (i, 0)),
            whole,
            pl.BlockSpec((3, features), lambda i: (0, 0)),
            whole,
        ],
        out_specs=[
            pl.BlockSpec((1, group_size, tokens, features), lambda i: (i, 0, 0, 0)),
            whole,
            pl.BlockSpec((1, features), lambda i: (0, 0)),
        ],
        out_shape=[
            jax.ShapeDtypeStruct((3, group_size, tokens, features), BF),
            jax.ShapeDtypeStruct((tokens, features), F32),
            jax.ShapeDtypeStruct((1, features), F32),
        ],
        scratch_shapes=[pltpu.VMEM((tokens, features), F32)],
        compiler_params=PARAMS,
        name="qkv_bwd",
    )(*packs, self_full, stream, gains, self_in_grad)


def feed_wgrad_kernel(group_size, split, owner_ref, *refs):
    hgu_refs = refs[:group_size]
    n3_refs = refs[group_size : 2 * group_size]
    cot_refs = refs[2 * group_size : 3 * group_size]
    out_ref = refs[3 * group_size]
    rows = out_ref.shape[1]
    start = (owner_ref[pl.program_id(0)] * group_size + owner_ref[pl.num_programs(0)]) * rows

    def product(right_refs, mask):
        total = None
        for left_ref, right_ref in zip(hgu_refs, right_refs):
            left = left_ref[...].reshape(rows, left_ref.shape[-1])
            if mask is not None:
                left = left * mask
            part = dot_nn(left, right_ref[...])
            total = part if total is None else total + part
        return total

    @pl.when(start + rows <= split)
    def _():
        out_ref[0] = product(n3_refs, None).astype(BF)

    @pl.when(start >= split)
    def _():
        out_ref[0] = product(cot_refs, None).astype(BF)

    @pl.when((start < split) & (start + rows > split))
    def _():
        row = start + lax.broadcasted_iota(jnp.int32, (rows, 1), 0)
        early = jnp.where(row < split, 1.0, 0.0).astype(F32)
        out_ref[0] = (
            product(n3_refs, None) * early + product(cot_refs, None) * (1.0 - early)
        ).astype(BF)


def run_feed_wgrad(owners, hgu, hgu_others, n3s, cots, rows):
    group_size = len(n3s)
    tokens, features = n3s[0].shape
    count = owners.shape[0] - 1
    whole = pl.BlockSpec((tokens, features), lambda i, o: (0, 0))
    return pl.pallas_call(
        functools.partial(feed_wgrad_kernel, group_size, 2 * F),
        grid_spec=pltpu.PrefetchScalarGridSpec(
            num_scalar_prefetch=1,
            grid=(count,),
            in_specs=[pl.BlockSpec((1, 1, rows, tokens), lambda i, o: (o[i], o[count], 0, 0))]
            + [pl.BlockSpec((1, rows, tokens), lambda i, o: (o[i], 0, 0))] * (group_size - 1)
            + [whole] * (2 * group_size),
            out_specs=pl.BlockSpec((1, rows, features), lambda i, o: (i, 0, 0)),
        ),
        out_shape=jax.ShapeDtypeStruct((count, rows, features), BF),
        compiler_params=PARAMS,
        name="feed_wgrad",
    )(owners, hgu, *hgu_others, *n3s, *cots)


def attn_wgrad_kernel(group_size, per_matrix, picks, owner_ref, *refs):
    out_ref = refs[-1]
    owner = owner_ref[pl.program_id(0)]
    matrix = owner // per_matrix
    block = owner % per_matrix
    for index, (lefts, rights) in enumerate(picks):

        @pl.when(matrix == index)
        def _():
            total = None
            for (left, piece), (right, where) in zip(lefts, rights):
                left_ref, right_ref = refs[left], refs[right]
                left_rows = left_ref[block] if piece is None else left_ref[block, owner_ref[pl.num_programs(0)]]
                part = dot_nn(left_rows, right_ref[where])
                total = part if total is None else total + part
            out_ref[0] = total.astype(BF)


def run_attn_wgrad(owners, picks, arrays, group_size, per_matrix, rows, features):
    count = owners.shape[0] - 1
    return pl.pallas_call(
        functools.partial(attn_wgrad_kernel, group_size, per_matrix, picks),
        grid_spec=pltpu.PrefetchScalarGridSpec(
            num_scalar_prefetch=1,
            grid=(count,),
            in_specs=[
                pl.BlockSpec(array.shape, lambda i, o, rank=array.ndim: (0,) * rank)
                for array in arrays
            ],
            out_specs=pl.BlockSpec((1, rows, features), lambda i, o: (i, 0, 0)),
        ),
        out_shape=jax.ShapeDtypeStruct((count, rows, features), BF),
        compiler_params=PARAMS,
        name="attn_wgrad",
    )(owners, *arrays)


def bit_reverse(value, bits):
    return int(format(value, f"0{bits}b")[::-1], 2) if bits else 0


def local(
    stream, encoder, self_weights, cross_weights, feed_weights,
    norm_gains, bias_table, bucket_onehot, key_keep, out_grad,
):
    group_size = lax.axis_size("seq")
    group_pos = lax.axis_index("seq")
    shard_count = lax.axis_size("fsdp")
    shard_pos = lax.axis_index("fsdp")
    shard_bits = shard_count.bit_length() - 1
    seq_count, tokens, features = stream.shape
    assert seq_count == 1
    enc_piece = encoder.shape[1]
    enc_len = enc_piece * group_size
    full_len = tokens * group_size
    per_matrix = shard_count // 4
    attn_rows = self_weights.shape[0] // group_size
    feed_rows = feed_weights.shape[0] // group_size

    stream = stream[0]
    out_grad = out_grad[0]
    encoder = encoder[0]

    def from_peer(values, offset):
        return lax.ppermute(
            values, "seq", [(i, (i - offset) % group_size) for i in range(group_size)]
        )

    def exchange(values):
        return [from_peer(values, d) for d in range(1, group_size)]

    def exchange_rows(values):
        return [
            from_peer(
                lax.dynamic_index_in_dim(values, (group_pos - d) % group_size, 1, keepdims=False), d
            )
            for d in range(1, group_size)
        ]

    enc_all = lax.dynamic_update_slice_in_dim(
        jnp.zeros((enc_len, features), BF), encoder, group_pos * enc_piece, 0
    )
    for d, piece in enumerate(exchange(encoder), 1):
        enc_all = lax.dynamic_update_slice_in_dim(
            enc_all, piece, ((group_pos + d) % group_size) * enc_piece, 0
        )
    cot_low = out_grad.astype(BF)
    cots = [cot_low] + exchange(cot_low)

    self_full = lax.all_gather(self_weights, "fsdp", axis=0, tiled=True)
    gains = lax.all_gather(norm_gains, "fsdp", axis=1, tiled=True).astype(F32)
    cross_full = lax.all_gather(cross_weights, "fsdp", axis=0, tiled=True)
    feed_full = lax.all_gather(feed_weights, "fsdp", axis=0, tiled=True)

    onehot = bucket_onehot.astype(F32)
    onehot_line = jnp.concatenate([onehot[:1], jnp.flip(onehot[1:], axis=0)], axis=0)
    bias_line = lax.dot_general(
        bias_table, onehot_line, (((1,), (1,)), ((), ())), precision=lax.Precision.HIGHEST
    )
    keep = key_keep.astype(F32)
    keep = lax.dynamic_slice_in_dim(
        jnp.concatenate([keep, keep], axis=1), group_pos * tokens, full_len, 1
    )
    pos = group_pos.astype(jnp.int32)[None]

    q, kv, n1t = run_qkv(stream, gains, self_full)
    kv_others = exchange(kv)
    prob, ctx, ctxt, after_self, n2, n2t = run_self_fwd(
        pos, q, kv, kv_others, keep, bias_line, stream, self_full, gains
    )
    cross_prob, cq, ckv, cctx, cctxt, after_cross, n3 = run_cross_fwd(
        after_self, n2, enc_all, cross_full, gains
    )

    def blocks(values):
        return values.reshape(-1, group_size, attn_rows, values.shape[-1])

    lefts = jnp.stack([blocks(n1t), blocks(ctxt), blocks(n2t), blocks(cctxt)])
    lefts = lefts.reshape(4 * per_matrix, group_size, attn_rows, tokens)
    left_others = exchange_rows(lefts)
    n3s = [n3] + exchange(n3)

    hgu, output, cross_in_grad, gain_three = run_feed(n3, out_grad, after_cross, gains, feed_full)
    hgu = hgu.reshape(shard_count, group_size, feed_rows, tokens)
    hgu_others = exchange_rows(hgu)

    order = [bit_reverse(p, shard_bits) for p in range(shard_count)]
    owners = jnp.array(order, jnp.int32) ^ shard_pos.astype(jnp.int32)
    half = shard_count // 2
    owners_keep = jnp.concatenate([owners[:half], pos])
    owners_send = jnp.concatenate([owners[half:], pos])

    def swap(values, bit):
        return lax.ppermute(values, "fsdp", [(i, i ^ (1 << bit)) for i in range(shard_count)])

    def scatter_sum(product):
        got = swap(product(owners_send), 0)
        kept = product(owners_keep)
        for bit in range(1, shard_bits):
            size = kept.shape[0] // 2
            send = (kept[size:].astype(F32) + got[size:].astype(F32)).astype(BF)
            moved = swap(send, bit)
            kept = kept[:size].astype(F32) + got[:size].astype(F32)
            got = moved
        return (kept.astype(F32) + got.astype(F32))[0]

    feed_grad = scatter_sum(
        lambda owners: run_feed_wgrad(owners, hgu, hgu_others, n3s, cots, feed_rows)
    )

    cross_pack, enc_pack, self_in_grad, gain_two = run_cross_bwd(
        cross_in_grad, cross_full, cross_prob, cctx, cq, ckv, after_self, gains
    )
    cross_others = exchange(cross_pack)
    enc_sum = enc_pack.astype(F32)
    for piece in exchange(enc_pack):
        enc_sum = enc_sum + piece.astype(F32)
    enc_sum = enc_sum.astype(BF)

    self_pack, dist_grad = run_self_bwd(cross_pack, self_full, prob, ctx, q, kv, kv_others)
    self_others = exchange(self_pack)

    def own_rows(values):
        return lax.dynamic_index_in_dim(values, group_pos, 1, keepdims=False)

    left_own = own_rows(lefts)
    left_list = [left_own] + left_others
    pieces = range(group_size)
    encT = enc_all.T.reshape(-1, group_size, attn_rows, enc_len)
    enc_rows = own_rows(encT)

    def take(which):
        return [piece[which * per_matrix : (which + 1) * per_matrix] for piece in left_list]

    cross_packs = [cross_pack] + cross_others
    cross_arrays = take(2) + take(3) + [enc_rows] + cross_packs + [enc_sum]
    g = group_size
    cross_picks = (
        (tuple((i, None) for i in pieces), tuple((2 * g + 1 + i, 1) for i in pieces)),
        (((2 * g, None),), ((3 * g + 1, 0),)),
        (((2 * g, None),), ((3 * g + 1, 1),)),
        (tuple((g + i, None) for i in pieces), tuple((2 * g + 1 + i, 0) for i in pieces)),
    )
    cross_grad = scatter_sum(
        lambda owners: run_attn_wgrad(
            owners, cross_picks, cross_arrays, g, per_matrix, attn_rows, features
        )
    )
    enc_own = lax.dynamic_slice_in_dim(enc_sum, group_pos * enc_piece, enc_piece, 1)
    encoder_grad = dot_nt(enc_own[0], cross_full[features : 2 * features]) + dot_nt(
        enc_own[1], cross_full[2 * features : 3 * features]
    )

    sums, stream_grad, gain_one = run_qkv_bwd(
        [self_pack] + self_others, self_full, stream, gains, self_in_grad
    )
    self_arrays = take(0) + take(1) + [sums[0], sums[1], sums[2]] + cross_packs
    self_picks = tuple(
        (tuple((i, None) for i in pieces), tuple((2 * g + m, i) for i in pieces)) for m in range(3)
    ) + ((tuple((g + i, None) for i in pieces), tuple((2 * g + 3 + i, 2) for i in pieces)),)
    self_grad = scatter_sum(
        lambda owners: run_attn_wgrad(
            owners, self_picks, self_arrays, g, per_matrix, attn_rows, features
        )
    )

    table_grad = jnp.dot(dist_grad, onehot_line, precision=lax.Precision.HIGHEST)
    table_flat = jnp.pad(table_grad.reshape(1, -1), ((0, 0), (0, features - table_grad.size)))
    small = jnp.concatenate([gain_one, gain_two, gain_three, table_flat], axis=0)
    for bit in range(shard_bits):
        small = small + swap(small, bit)
    step = 1
    while step < group_size:
        small = small + lax.ppermute(small, "seq", [(i, i ^ step) for i in range(group_size)])
        step *= 2
    return (
        output[None],
        stream_grad[None],
        encoder_grad[None],
        small[:3],
        small[3, : table_grad.size].reshape(table_grad.shape),
        self_grad,
        cross_grad,
        feed_grad,
    )


def solution(mesh):
    placed = (
        P("fsdp", "seq", None),
        P("fsdp", "seq", None),
        P("fsdp", None),
        P("fsdp", None),
        P("fsdp", None),
        P(None, "fsdp"),
        P(),
        P(),
        P("fsdp", None),
        P("fsdp", "seq", None),
    )
    return jax.shard_map(
        local,
        mesh=mesh,
        in_specs=placed,
        out_specs=(
            P("fsdp", "seq", None),
            P("fsdp", "seq", None),
            P("fsdp", "seq", None),
            P(),
            P(),
            P(("fsdp", "seq"), None),
            P(("fsdp", "seq"), None),
            P(("fsdp", "seq"), None),
        ),
        check_vma=False,
    )
```

time: 599 us -> 464 us (0.77); the launches traced: 587 us -> 462 us
  waiting for transfers between devices: 125 us -> 282 us
  blocking collectives: 155 us -> 21.9 us
  Pallas kernels: 0 us -> 87.9 us
  matrix products: 80.1 us -> 2.63 us
  local copies, waits for them, and re-layouts: 88.1 us -> 13.3 us
  other arithmetic: 58 us -> 14.8 us
  starting transfers between devices: 64.4 us -> 25.1 us
    ppermute x0 -> x26, waiting for transfers between devices: none -> 142 us  [the longest x16 71.9 us: swap(): lax.ppermute(values, 'fsdp', [(i, i ^ 1 << bit) for i in range(shard_coun...]
    pallas_call x0 -> x13, Pallas kernels: none -> 87.9 us  [the longest x4 24.9 us: run_attn_wgrad(): pl.pallas_call(functools.partial(attn_wgrad_kernel, group_size, per_matri...]
    all_gather x6 -> x3, waiting for transfers between devices: 51.5 us -> 138 us  [the longest x1 76 us: local(): feed_full = lax.all_gather(feed_weights, 'fsdp', axis=0, tiled=True)]
    all_gather x10 -> x1, blocking collectives: 105 us -> 21.9 us  [local(): gains = lax.all_gather(norm_gains, 'fsdp', axis=1, tiled=True).astype(F32)]
    dot_general x47 -> x4, matrix products: 80.1 us -> 2.63 us  [the longest x2 1.6 us: dot_nt(): lax.dot_general(a, b, (((1,), (1,)), ((), ())), preferred_element_type=F32)]
    all_to_all x18 -> x0, starting transfers between devices: 63.4 us -> none  [the longest x1 4.33 us: local(): lax.all_to_all(sk_grad_heads, 'seq', split_axis=1, concat_axis=2, tiled=T...]
    reduce_scatter x3 -> x0, waiting for transfers between devices: 58.7 us -> none  [the longest x1 58.7 us: local(): lax.psum_scatter(feed_slab, 'fsdp', scatter_dimension=0, tiled=True)]
    psum x1 -> x0, blocking collectives: 42 us -> none  [local(): lax.psum((gain_grads, table_full), ('fsdp', 'seq'))]
  transfers between devices with their start and end apart: 27 -> 29, of which waited for: 12 -> 14; matrix products, arithmetic and copies ran while one was open for 35% -> 5% of each run, Pallas kernels for 0% -> 15%
where the time goes in v1:
time: 464 us; the launch traced here: 462 us
  waiting for transfers between devices  282 us (61%)
  Pallas kernels  87.9 us (19%)
  starting transfers between devices  25.1 us (5%)
  blocking collectives  21.9 us (5%)
  other arithmetic  14.8 us (3%)
  between operations  14.2 us (3%)
  local copies, waits for them, and re-layouts  13.3 us (3%)
    all_gather x1, waiting for transfers between devices, local(): feed_full = lax.all_gather(feed_weights, 'fsdp', axis=0, tiled=True)  76 us
    ppermute x16, waiting for transfers between devices, swap(): lax.ppermute(values, 'fsdp', [(i, i ^ 1 << bit) for i in range(shard_coun...  71.9 us
    ppermute x9, waiting for transfers between devices, from_peer(): lax.ppermute(values, 'seq', [(i, (i - offset) % group_size) for i in rang...  68.2 us
    all_gather x1, waiting for transfers between devices, local(): cross_full = lax.all_gather(cross_weights, 'fsdp', axis=0, tiled=True)  31.5 us
    all_gather x1, waiting for transfers between devices, local(): self_full = lax.all_gather(self_weights, 'fsdp', axis=0, tiled=True)  30.7 us
    pallas_call x4, Pallas kernels, run_attn_wgrad(): pl.pallas_call(functools.partial(attn_wgrad_kernel, group_size, per_matri...  24.9 us
    all_gather x1, blocking collectives, local(): gains = lax.all_gather(norm_gains, 'fsdp', axis=1, tiled=True).astype(F32)  21.9 us
    pallas_call x2, Pallas kernels, run_feed_wgrad(): pl.pallas_call(functools.partial(feed_wgrad_kernel, group_size, 2 * F), g...  14.7 us
  transfers between devices with their start and end apart: 29, of which 14 were waited for; matrix products, arithmetic and copies ran while one was open for 5% of the time, Pallas kernels for 15%

profile of v1, /device:TPU:0, one launch (start us, length us, event | category | flops | bytes accessed | tf_op | source)
XLA Modules:
  0.0 462.1 jit_solution(8498114855390755779)
XLA Ops:
  9.5 3.1 collective-permute-start.1
  12.6 21.9 %all-gather = bf16[16,48,3]{1,2,0:T(4,128)(2,1)S(1)} all-gather(bf16[1,48,3]{1,2,0:T(4,128)(2,1)S(1)} %bitcast.89), channel_id=1, replica_groups=mesh['fsdp'=16,'seq'=2] {'fsdp'}, dimensions={0}, use_global_device_ids=true | all-gather | bytes 4896 | tf_op jit(solution)/shard_map/all_gather | solution.py:639
  35.5 30.7 %all-gather.5.cloned.1.call-done.w_ref.refs_7_.refs_1_.refs_2_ = bf16[3072,768]{1,0:T(8,128)(2,1)} async-done(((bf16[192,768]{1,0:T(8,128)(2,1)}), bf16[3072,768]{1,0:T(8,128)(2,1)}) %all-gather.5.cloned.1.call-update) | async-done | bytes 4718608 | tf_op jit(solution)/shard_map/all_gather | solution.py:638
  66.2 4.4 qkv.1
  70.6 1.5 collective-permute-start
  73.5 8.6 %collective-permute-done.refs_3_.refs_6_ = bf16[2,128,768]{2,1,0:T(8,128)(2,1)S(1)} collective-permute-done((bf16[2,128,768]{2,1,0:T(8,128)(2,1)}, bf16[2,128,768]{2,1,0:T(8,128)(2,1)S(1)}, u32[]{:S(2)}, u32[]{:S(2)}) %collective-permute-start) | collective-permute-done | bytes 393248 | tf_op jit(solution)/shard_map/ppermute | solution.py:613
  82.9 5.8 %self_fwd.1 = (f32[12,128,256]{2,1,0:T(8,128)}, bf16[128,768]{1,0:T(8,128)(2,1)}, bf16[768,128]{1,0:T(8,128)(2,1)}, f32[128,768]{1,0:T(8,128)}, bf16[128,768]{1,0:T(8,128)(2,1)}, /*index=5*/bf16[768,128]{1,0:T(8,128)(2,1)}) custom-call(s32[1]{0:T(128)} %bitcast.refs_0_, bf16[128,768]{1,0:T(8,128)(2,1)} %get-tuple-element.37.refs_1_.refs_4_, ...), custom_call_target="tpu_custom_call" | custom-call | tf_op jit(solution)/shard_map/self_fwd/pallas_call | solution.py:157
  88.7 31.5 %all-gather.7.cloned.1.call-done.w_ref = bf16[3072,768]{1,0:T(8,128)(2,1)} async-done(((bf16[192,768]{1,0:T(8,128)(2,1)}), bf16[3072,768]{1,0:T(8,128)(2,1)}) %all-gather.7.cloned.1.call-update) | async-done | bytes 4718608 | tf_op jit(solution)/shard_map/all_gather | solution.py:640
  120.2 5.8 %cross_fwd.1 = (f32[12,128,64]{2,1,0:T(8,128)}, bf16[128,768]{1,0:T(8,128)(2,1)}, bf16[2,64,768]{2,1,0:T(8,128)(2,1)}, bf16[128,768]{1,0:T(8,128)(2,1)}, bf16[76...) custom-call(f32[128,768]{1,0:T(8,128)} %get-tuple-element.39.after_ref, ...), custom_call_target="tpu_custom_call" | custom-call | tf_op jit(solution)/shard_map/cross_fwd/pallas_call | solution.py:210
  126.0 76.0 %all-gather.9.cloned.1.call-done.g0_ref.g1_ref.g2_ref = bf16[6144,768]{1,0:T(8,128)(2,1)} async-done(((bf16[384,768]{1,0:T(8,128)(2,1)}), bf16[6144,768]{1,0:T(8,128)(2,1)}) %all-gather.9.cloned.1.call-update) | async-done | bytes 9437200 | tf_op jit(solution)/shard_map/all_gather | solution.py:641
  202.0 12.0 %feed.1 = (bf16[3,2048,128]{2,1,0:T(8,128)(2,1)}, f32[128,768]{1,0:T(8,128)}, f32[128,768]{1,0:T(8,128)}, f32[1,768]{1,0:T(1,128)}) custom-call(bf16[128,768]{1,0:T(8,128)(2,1)} %get-tuple-element.41.n3_ref.refs_2_, f32[128,768]{1,0:T(8,128)} %bitcast.72, f32[128,768]{1,0:T(8,128)} %get-tuple-element.42.after_ref, f32[3,768]{1,0:T(4,128)} %bitcast.79, ...), custom_call_target="tpu_custom_call" | custom-call | tf_op jit(solution)/shard_map/feed/pallas_call | solution.py:276
  214.1 2.2 dynamic-slice_bitcast_fusion
  216.3 1.5 collective-permute-start.19
  218.5 1.5 collective-permute-start.20
  220.8 20.3 %collective-permute-done.21.refs_5_ = bf16[128,768]{1,0:T(8,128)(2,1)S(1)} collective-permute-done((bf16[128,768]{1,0:T(8,128)(2,1)S(1)}, bf16[128,768]{1,0:T(8,128)(2,1)S(1)}, u32[]{:S(2)}, u32[]{:S(2)}) %collective-permute-start.21) | collective-permute-done | bytes 196640 | tf_op jit(solution)/shard_map/ppermute | solution.py:613
  241.1 3.5 collective-permute-done.20.refs_3_
  246.2 7.3 %feed_wgrad.3 = bf16[8,192,768]{2,1,0:T(8,128)(2,1)} custom-call(s32[9]{0:T(128)} %pad_add_fusion.1.owner_ref, bf16[16,2,192,128]{3,2,1,0:T(8,128)(2,1)} %bitcast.65, bf16[16,192,128]{2,1,0:T(8,128)(2,1)} %copy-done.7, bf16[128,768]{1,0:T(8,128)(2,1)} %get-tuple-element.41.n3_ref.refs_2_, bf16[128,768]{1,0:T(8,128)(2,1)} %copy-done.17, ...), custom_call_target="tpu_custom_call" | custom-call | tf_op jit(solution)/shard_map/feed_wgrad/pallas_call | solution.py:533
  253.6 1.6 collective-permute-start.9
  255.1 7.1 %cross_bwd.1 = (bf16[3,128,768]{2,1,0:T(8,128)(2,1)}, bf16[2,64,768]{2,1,0:T(8,128)(2,1)}, f32[128,768]{1,0:T(8,128)}, f32[1,768]{1,0:T(1,128)}) custom-call(f32[128,768]{1,0:T(8,128)} %get-tuple-element.44.in_grad_ref, bf16[3072,768]{1,0:T(8,128)(2,1)} %all-gather.7.cloned.1.call-done.w_ref, f32[12,128,64]{2,1,0:T(8,128)} %get-tuple-element.45.prob_ref, ...), custom_call_target="tpu_custom_call" | custom-call | tf_op jit(solution)/shard_map/cross_bwd/pallas_call | solution.py:346
  262.2 7.4 %self_bwd.1 = (bf16[5,128,768]{2,1,0:T(8,128)(2,1)}, f32[12,256]{1,0:T(8,128)}) custom-call(bf16[3,128,768]{2,1,0:T(8,128)(2,1)} %get-tuple-element.49.refs_0_.refs_7_.refs_5_, bf16[3072,768]{1,0:T(8,128)(2,1)} %all-gather.5.cloned.1.call-done.w_ref.refs_7_.refs_1_.refs_2_, f32[12,128,256]{2,1,0:T(8,128)} %get-tuple-element.50.refs_2_, ...), custom_call_target="tpu_custom_call" | custom-call | tf_op jit(solution)/shard_map/self_bwd/pallas_call | solution.py:414
  271.2 1.5 collective-permute-start.10
  274.8 35.8 %collective-permute-done.3 = bf16[2,64,768]{2,1,0:T(8,128)(2,1)S(1)} collective-permute-done((bf16[2,64,768]{2,1,0:T(8,128)(2,1)}, bf16[2,64,768]{2,1,0:T(8,128)(2,1)S(1)}, u32[]{:S(2)}, u32[]{:S(2)}) %collective-permute-start.3) | collective-permute-done | bytes 196640 | tf_op jit(solution)/shard_map/ppermute | solution.py:613
  312.1 6.1 %attn_wgrad.7 = bf16[8,96,768]{2,1,0:T(8,128)(2,1)} custom-call(s32[9]{0:T(128)} %pad_add_fusion.1.owner_ref, bf16[4,96,128]{2,1,0:T(8,128)(2,1)} %get-tuple-element.82.refs_0_, bf16[4,96,128]{2,1,0:T(8,128)(2,1)} %get-tuple-element.86.refs_1_, bf16[4,96,128]{2,1,0:T(8,128)(2,1)} %get-tuple-element.81.refs_2_, ...), custom_call_target="tpu_custom_call" | custom-call | tf_op jit(solution)/shard_map/attn_wgrad/pallas_call | solution.py:569
  318.5 1.0 copy-done.13
  319.5 5.8 %qkv_bwd.1 = (bf16[3,2,128,768]{3,2,1,0:T(8,128)(2,1)}, f32[128,768]{1,0:T(8,128)}, f32[1,768]{1,0:T(1,128)}) custom-call(bf16[5,128,768]{2,1,0:T(8,128)(2,1)} %get-tuple-element.52.refs_0_, bf16[5,128,768]{2,1,0:T(8,128)(2,1)} %copy-done.13, bf16[3072,768]{1,0:T(8,128)(2,1)} %all-gather.5.cloned.1.call-done.w_ref.refs_7_.refs_1_.refs_2_, ...), custom_call_target="tpu_custom_call" | custom-call | tf_op jit(solution)/shard_map/qkv_bwd/pallas_call | solution.py:467
  326.5 2.3 slice_bitcast_fusion
  328.8 6.5 %attn_wgrad.5 = bf16[8,96,768]{2,1,0:T(8,128)(2,1)} custom-call(s32[9]{0:T(128)} %pad_add_fusion.1.owner_ref, bf16[4,96,128]{2,1,0:T(8,128)(2,1)} %get-tuple-element.84.refs_0_, bf16[4,96,128]{2,1,0:T(8,128)(2,1)} %get-tuple-element.88.refs_1_, bf16[4,96,128]{2,1,0:T(8,128)(2,1)} %get-tuple-element.83.refs_2_, ...), custom_call_target="tpu_custom_call" | custom-call | tf_op jit(solution)/shard_map/attn_wgrad/pallas_call | solution.py:569
  335.9 3.1 collective-permute-done.5
  339.1 1.0 collective-permute-start.6
  340.7 5.9 %attn_wgrad.6 = bf16[8,96,768]{2,1,0:T(8,128)(2,1)} custom-call(s32[9]{0:T(128)} %pad_add_fusion.owner_ref, bf16[4,96,128]{2,1,0:T(8,128)(2,1)} %get-tuple-element.82.refs_0_, bf16[4,96,128]{2,1,0:T(8,128)(2,1)} %get-tuple-element.86.refs_1_, bf16[4,96,128]{2,1,0:T(8,128)(2,1)} %get-tuple-element.81.refs_2_, bf16[4,96,128]{2,1,0:T(8,128)(2,1)} %get-tuple-element.85.refs_3_, ...), custom_call_target="tpu_custom_call" | custom-call | tf_op jit(solution)/shard_map/attn_wgrad/pallas_call | solution.py:569
  346.6 7.4 %feed_wgrad.2 = bf16[8,192,768]{2,1,0:T(8,128)(2,1)} custom-call(s32[9]{0:T(128)} %pad_add_fusion.owner_ref, bf16[16,2,192,128]{3,2,1,0:T(8,128)(2,1)} %bitcast.66, bf16[16,192,128]{2,1,0:T(8,128)(2,1)} %copy-done.7, bf16[128,768]{1,0:T(8,128)(2,1)} %get-tuple-element.41.n3_ref.refs_2_, bf16[128,768]{1,0:T(8,128)(2,1)} %copy-done.17, ...), custom_call_target="tpu_custom_call" | custom-call | tf_op jit(solution)/shard_map/feed_wgrad/pallas_call | solution.py:533
  354.0 6.5 %attn_wgrad.4 = bf16[8,96,768]{2,1,0:T(8,128)(2,1)} custom-call(s32[9]{0:T(128)} %pad_add_fusion.owner_ref, bf16[4,96,128]{2,1,0:T(8,128)(2,1)} %get-tuple-element.84.refs_0_, bf16[4,96,128]{2,1,0:T(8,128)(2,1)} %get-tuple-element.88.refs_1_, bf16[4,96,128]{2,1,0:T(8,128)(2,1)} %get-tuple-element.83.refs_2_, bf16[4,96,128]{2,1,0:T(8,128)(2,1)} %get-tuple-element.87.refs_3_, ...), custom_call_target="tpu_custom_call" | custom-call | tf_op jit(solution)/shard_map/attn_wgrad/pallas_call | solution.py:569
  360.5 1.3 collective-permute-start.7
  362.8 2.8 add_convert_fusion
  365.6 1.2 collective-permute-start.23
  367.0 1.0 collective-permute-start.12
  369.2 1.1 fusion.8
  370.4 1.9 collective-permute-done.8
  372.3 6.2 %collective-permute-done.16 = bf16[4,96,768]{2,1,0:T(8,128)(2,1)S(1)} collective-permute-done((bf16[4,96,768]{2,1,0:T(8,128)(2,1)S(1)}, bf16[4,96,768]{2,1,0:T(8,128)(2,1)S(1)}, u32[]{:S(2)}, u32[]{:S(2)}) %collective-permute-start.16) | collective-permute-done | bytes 589856 | tf_op jit(solution)/shard_map/ppermute | solution.py:682
  379.3 1.3 collective-permute-start.17
  380.6 33.5 %collective-permute-done.12 = bf16[4,96,768]{2,1,0:T(8,128)(2,1)S(1)} collective-permute-done((bf16[4,96,768]{2,1,0:T(8,128)(2,1)S(1)}, bf16[4,96,768]{2,1,0:T(8,128)(2,1)S(1)}, u32[]{:S(2)}, u32[]{:S(2)}) %collective-permute-start.12) | collective-permute-done | bytes 589856 | tf_op jit(solution)/shard_map/ppermute | solution.py:682
  415.0 1.3 collective-permute-start.13
  418.9 1.7 collective-permute-start.18
  420.7 9.2 %collective-permute-done.13 = bf16[2,96,768]{2,1,0:T(8,128)(2,1)} collective-permute-done((bf16[2,96,768]{2,1,0:T(8,128)(2,1)}, bf16[2,96,768]{2,1,0:T(8,128)(2,1)}, u32[]{:S(2)}, u32[]{:S(2)}) %collective-permute-start.13) | collective-permute-done | bytes 294944 | tf_op jit(solution)/shard_map/ppermute | solution.py:682
  431.1 9.8 %collective-permute-done.24 = bf16[2,192,768]{2,1,0:T(8,128)(2,1)S(1)} collective-permute-done((bf16[2,192,768]{2,1,0:T(8,128)(2,1)S(1)}, bf16[2,192,768]{2,1,0:T(8,128)(2,1)S(1)}, u32[]{:S(2)}, u32[]{:S(2)}) %collective-permute-start.24) | collective-permute-done | bytes 589856 | tf_op jit(solution)/shard_map/ppermute | solution.py:682
  441.2 1.7 fusion.18
  442.9 1.7 fusion.21
  444.6 10.0 %collective-permute-done.25 = bf16[1,192,768]{2,1,0:T(8,128)(2,1)S(1)} collective-permute-done((bf16[1,192,768]{2,1,0:T(8,128)(2,1)S(1)}, bf16[1,192,768]{2,1,0:T(8,128)(2,1)S(1)}, u32[]{:S(2)}, u32[]{:S(2)}) %collective-permute-start.25) | collective-permute-done | bytes 294944 | tf_op jit(solution)/shard_map/ppermute | solution.py:682
  (155 shorter events, 25.8 us)
Async XLA Ops:
  7.2 64.9 %copy-start = (f32[12,32]{1,0:T(8,128)S(1)}, f32[12,32]{1,0:T(8,128)}, u32[]{:S(2)}) copy-start(f32[12,32]{1,0:T(8,128)} %param.17) | copy-start | bytes 4612
  7.2 59.0 %all-gather.5.cloned.1.call-start = ((), (), s32[]{:S(2)}) async-start(), calls=%async_computation | async-start | bytes 5013504 | tf_op jit(solution)/shard_map/all_gather | solution.py:638
  8.0 112.2 %all-gather.7.cloned.1.call-start = ((), (), s32[]{:S(2)}) async-start(), calls=%async_computation.1 | async-start | bytes 5013504 | tf_op jit(solution)/shard_map/all_gather | solution.py:640
  8.7 193.2 %all-gather.9.cloned.1.call-start = ((), (), s32[]{:S(2)}) async-start(), calls=%async_computation.2 | async-start | bytes 10027008 | tf_op jit(solution)/shard_map/all_gather | solution.py:641
  9.5 64.0 %collective-permute-start.1 = (bf16[32,768]{1,0:T(8,128)(2,1)S(1)}, bf16[32,768]{1,0:T(8,128)(2,1)S(1)}, u32[]{:S(2)}, u32[]{:S(2)}) collective-permute-start(bf16[32,768]{1,0:T(8,128)(2,1)S(1)} %bitcast.87), channel_id=1, source_target_pairs={{0,1},{1,0},{2,3},{3,2},{4,5},{5,4},{6,7},{7,6},{8,9},{9,8},{10,11... | collective-permute-start | bytes 147464 | tf_op jit(solution)/shard_map/ppermute | solution.py:613
  12.6 59.5 %copy-start.23 = (f32[1,32]{0,1:T(8,128)}, f32[1,32]{0,1:T(8,128)S(1)}, u32[]{:S(2)}) copy-start(f32[1,32]{0,1:T(8,128)S(1)} %slice.244) | copy-start | bytes 388
  70.6 11.5 %collective-permute-start = (bf16[2,128,768]{2,1,0:T(8,128)(2,1)}, bf16[2,128,768]{2,1,0:T(8,128)(2,1)S(1)}, u32[]{:S(2)}, u32[]{:S(2)}) collective-permute-start(bf16[2,128,768]{2,1,0:T(8,128)(2,1)} %get-tuple-element.38.refs_2_.refs_5_), channel_id=1, source_target_pairs={{0,1},{1,0},{2,3},{3,2},{4,5},{5,4},{6,7},{7,6},{8,9},{9,8},{10,11... | collective-permute-start | bytes 1179656 | tf_op jit(solution)/shard_map/ppermute | solution.py:613
  73.5 46.7 %copy-start.14 = (bf16[64,768]{1,0:T(8,128)(2,1)}, bf16[64,768]{1,0:T(8,128)(2,1)S(1)}, u32[]{:S(2)}) copy-start(bf16[64,768]{1,0:T(8,128)(2,1)S(1)} %constant_dynamic-update-slice_fusion.enc_ref) | copy-start | bytes 294916
  214.0 6.5 %copy-start.18 = (bf16[768,128]{1,0:T(8,128)(2,1)S(1)}, bf16[768,128]{1,0:T(8,128)(2,1)}, u32[]{:S(2)}) copy-start(bf16[768,128]{1,0:T(8,128)(2,1)} %get-tuple-element.60) | copy-start | bytes 589828
  214.1 6.5 %copy-start.19 = (bf16[768,128]{1,0:T(8,128)(2,1)S(1)}, bf16[768,128]{1,0:T(8,128)(2,1)}, u32[]{:S(2)}) copy-start(bf16[768,128]{1,0:T(8,128)(2,1)} %get-tuple-element.61) | copy-start | bytes 589828
  214.1 6.5 %copy-start.20 = (bf16[768,128]{1,0:T(8,128)(2,1)S(1)}, bf16[768,128]{1,0:T(8,128)(2,1)}, u32[]{:S(2)}) copy-start(bf16[768,128]{1,0:T(8,128)(2,1)} %get-tuple-element.62) | copy-start | bytes 589828
  214.1 6.5 %copy-start.21 = (bf16[768,128]{1,0:T(8,128)(2,1)S(1)}, bf16[768,128]{1,0:T(8,128)(2,1)}, u32[]{:S(2)}) copy-start(bf16[768,128]{1,0:T(8,128)(2,1)} %get-tuple-element.63) | copy-start | bytes 589828
  216.3 28.3 %collective-permute-start.19 = (bf16[16,192,128]{2,1,0:T(8,128)(2,1)}, bf16[16,192,128]{2,1,0:T(8,128)(2,1)S(1)}, u32[]{:S(2)}, u32[]{:S(2)}) collective-permute-start(bf16[16,192,128]{2,1,0:T(8,128)(2,1)} %dynamic-slice_bitcast_fusion), channel_id=1, source_target_pairs={{0,1},{1,0},{2,3},{3,2},{4,5},{5,4},{6,7},{7,6},{8,9},{9,8},{10,11... | collective-permute-start | bytes 2359304 | tf_op jit(solution)/shard_map/ppermute | solution.py:613
  217.8 23.3 %collective-permute-start.21 = (bf16[128,768]{1,0:T(8,128)(2,1)S(1)}, bf16[128,768]{1,0:T(8,128)(2,1)S(1)}, u32[]{:S(2)}, u32[]{:S(2)}) collective-permute-start(bf16[128,768]{1,0:T(8,128)(2,1)S(1)} %bitcast_convert_fusion.refs_4_), channel_id=1, source_target_pairs={{0,1},{1,0},{2,3},{3,2},{4,5},{5,4},{6,7},{7,6},{8,9},{9,8},{10,11... | collective-permute-start | bytes 589832 | tf_op jit(solution)/shard_map/ppermute | solution.py:613
  218.5 26.1 %collective-permute-start.20 = (bf16[128,768]{1,0:T(8,128)(2,1)S(1)}, bf16[128,768]{1,0:T(8,128)(2,1)S(1)}, u32[]{:S(2)}, u32[]{:S(2)}) collective-permute-start(bf16[128,768]{1,0:T(8,128)(2,1)S(1)} %copy-done.9), channel_id=1, source_target_pairs={{0,1},{1,0},{2,3},{3,2},{4,5},{5,4},{6,7},{7,6},{8,9},{9,8},{10,11... | collective-permute-start | bytes 589832 | tf_op jit(solution)/shard_map/ppermute | solution.py:613
  253.5 109.2 %collective-permute-start.22 = (bf16[8,192,768]{2,1,0:T(8,128)(2,1)}, bf16[8,192,768]{2,1,0:T(8,128)(2,1)}, u32[]{:S(2)}, u32[]{:S(2)}) collective-permute-start(bf16[8,192,768]{2,1,0:T(8,128)(2,1)} %feed_wgrad.3), channel_id=1, source_target_pairs={{0,2},{2,0},{4,6},{6,4},{8,10},{10,8},{12,14},{14,12},{16,18},{18,... | collective-permute-start | bytes 7077896 | tf_op jit(solution)/shard_map/ppermute | solution.py:682
  253.6 20.4 %collective-permute-start.9 = (bf16[16,96,128]{2,1,0:T(8,128)(2,1)S(1)}, bf16[16,96,128]{2,1,0:T(8,128)(2,1)S(1)}, u32[]{:S(2)}, u32[]{:S(2)}) collective-permute-start(bf16[16,96,128]{2,1,0:T(8,128)(2,1)S(1)} %dynamic-slice_bitcast_fusion.1), channel_id=1, source_target_pairs={{0,1},{1,0},{2,3},{3,2},{4,5},{5,4},{6,7},{7,6},{8,9},{9,8},{10,11... | collective-permute-start | bytes 1179656 | tf_op jit(solution)/shard_map/ppermute | solution.py:613
  262.2 7.9 %copy-start.15 = (bf16[64,768]{1,0:T(8,128)(2,1)S(1)}, bf16[64,768]{1,0:T(8,128)(2,1)}, u32[]{:S(2)}) copy-start(bf16[64,768]{1,0:T(8,128)(2,1)} %copy-done.14) | copy-start | bytes 294916
  262.2 9.0 %copy-start.2 = (bf16[3,128,768]{2,1,0:T(8,128)(2,1)S(1)}, bf16[3,128,768]{2,1,0:T(8,128)(2,1)}, u32[]{:S(2)}) copy-start(bf16[3,128,768]{2,1,0:T(8,128)(2,1)} %get-tuple-element.49.refs_0_.refs_7_.refs_5_) | copy-start | bytes 1769476
  269.6 48.9 %collective-permute-start.2 = (bf16[5,128,768]{2,1,0:T(8,128)(2,1)}, bf16[5,128,768]{2,1,0:T(8,128)(2,1)S(1)}, u32[]{:S(2)}, u32[]{:S(2)}) collective-permute-start(bf16[5,128,768]{2,1,0:T(8,128)(2,1)} %get-tuple-element.52.refs_0_), channel_id=1, source_target_pairs={{0,1},{1,0},{2,3},{3,2},{4,5},{5,4},{6,7},{7,6},{8,9},{9,8},{10,11... | collective-permute-start | bytes 2949128 | tf_op jit(solution)/shard_map/ppermute | solution.py:613
  270.5 40.1 %copy-start.22 = (bf16[2,64,768]{2,1,0:T(8,128)(2,1)S(1)}, bf16[2,64,768]{2,1,0:T(8,128)(2,1)}, u32[]{:S(2)}) copy-start(bf16[2,64,768]{2,1,0:T(8,128)(2,1)} %get-tuple-element.55) | copy-start | bytes 589828
  271.2 40.1 %collective-permute-start.10 = (bf16[3,128,768]{2,1,0:T(8,128)(2,1)S(1)}, bf16[3,128,768]{2,1,0:T(8,128)(2,1)S(1)}, u32[]{:S(2)}, u32[]{:S(2)}) collective-permute-start(bf16[3,128,768]{2,1,0:T(8,128)(2,1)S(1)} %copy-done.2), channel_id=1, source_target_pairs={{0,1},{1,0},{2,3},{3,2},{4,5},{5,4},{6,7},{7,6},{8,9},{9,8},{10,11... | collective-permute-start | bytes 1769480 | tf_op jit(solution)/shard_map/ppermute | solution.py:613
  273.5 37.1 %collective-permute-start.3 = (bf16[2,64,768]{2,1,0:T(8,128)(2,1)}, bf16[2,64,768]{2,1,0:T(8,128)(2,1)S(1)}, u32[]{:S(2)}, u32[]{:S(2)}) collective-permute-start(bf16[2,64,768]{2,1,0:T(8,128)(2,1)} %get-tuple-element.55), channel_id=1, source_target_pairs={{0,1},{1,0},{2,3},{3,2},{4,5},{5,4},{6,7},{7,6},{8,9},{9,8},{10,11... | collective-permute-start | bytes 589832 | tf_op jit(solution)/shard_map/ppermute | solution.py:613
  312.1 6.1 %copy-start.24 = (f32[1,32]{0,1:T(8,128)S(1)}, f32[1,32]{0,1:T(8,128)}, u32[]{:S(2)}) copy-start(f32[1,32]{0,1:T(8,128)} %copy-done.23) | copy-start | bytes 388
  312.1 6.1 %copy-start.30 = (f32[12,256]{1,0:T(8,128)S(1)}, f32[12,256]{1,0:T(8,128)}, u32[]{:S(2)}) copy-start(f32[12,256]{1,0:T(8,128)} %get-tuple-element.59) | copy-start | bytes 36868
  318.2 43.7 %collective-permute-start.15 = (bf16[8,96,768]{2,1,0:T(8,128)(2,1)}, bf16[8,96,768]{2,1,0:T(8,128)(2,1)S(1)}, u32[]{:S(2)}, u32[]{:S(2)}) collective-permute-start(bf16[8,96,768]{2,1,0:T(8,128)(2,1)} %attn_wgrad.7), channel_id=1, source_target_pairs={{0,2},{2,0},{4,6},{6,4},{8,10},{10,8},{12,14},{14,12},{16,18},{18,... | collective-permute-start | bytes 3538952 | tf_op jit(solution)/shard_map/ppermute | solution.py:682
  319.5 5.8 %copy-start.28 = (f32[1,768]{1,0:T(1,128)S(1)}, f32[1,768]{1,0:T(1,128)}, u32[]{:S(2)}) copy-start(f32[1,768]{1,0:T(1,128)} %get-tuple-element.57) | copy-start | bytes 9220
  326.0 9.3 %collective-permute-start.4 = (f32[4,768]{1,0:T(4,128)S(1)}, f32[4,768]{1,0:T(4,128)S(1)}, u32[]{:S(2)}, u32[]{:S(2)}) collective-permute-start(f32[4,768]{1,0:T(4,128)S(1)} %select_maximum_fusion), channel_id=1, source_target_pairs={{0,2},{2,0},{4,6},{6,4},{8,10},{10,8},{12,14},{14,12},{16,18},{18,... | collective-permute-start | bytes 36872 | tf_op jit(solution)/shard_map/ppermute | solution.py:682
  328.8 6.5 %copy-start.29 = (f32[1,768]{1,0:T(1,128)S(1)}, f32[1,768]{1,0:T(1,128)}, u32[]{:S(2)}) copy-start(f32[1,768]{1,0:T(1,128)} %get-tuple-element.56) | copy-start | bytes 9220
  335.3 31.4 %collective-permute-start.11 = (bf16[8,96,768]{2,1,0:T(8,128)(2,1)}, bf16[8,96,768]{2,1,0:T(8,128)(2,1)S(1)}, u32[]{:S(2)}, u32[]{:S(2)}) collective-permute-start(bf16[8,96,768]{2,1,0:T(8,128)(2,1)} %attn_wgrad.5), channel_id=1, source_target_pairs={{0,2},{2,0},{4,6},{6,4},{8,10},{10,8},{12,14},{14,12},{16,18},{18,... | collective-permute-start | bytes 3538952 | tf_op jit(solution)/shard_map/ppermute | solution.py:682
  335.3 3.8 collective-permute-start.5
  339.1 21.4 %collective-permute-start.6 = (f32[4,768]{1,0:T(4,128)S(1)}, f32[4,768]{1,0:T(4,128)S(1)}, u32[]{:S(2)}, u32[]{:S(2)}) collective-permute-start(f32[4,768]{1,0:T(4,128)S(1)} %fusion.33), channel_id=1, source_target_pairs={{0,8},{2,10},{4,12},{6,14},{8,0},{10,2},{12,4},{14,6},{16,24},{18,... | collective-permute-start | bytes 36872 | tf_op jit(solution)/shard_map/ppermute | solution.py:682
  354.0 7.8 %copy-start.5 = (bf16[8,96,768]{2,1,0:T(8,128)(2,1)S(1)}, bf16[8,96,768]{2,1,0:T(8,128)(2,1)}, u32[]{:S(2)}) copy-start(bf16[8,96,768]{2,1,0:T(8,128)(2,1)} %attn_wgrad.6) | copy-start | bytes 3538948
  360.5 7.9 %collective-permute-start.7 = (f32[4,768]{1,0:T(4,128)S(1)}, f32[4,768]{1,0:T(4,128)S(1)}, u32[]{:S(2)}, u32[]{:S(2)}) collective-permute-start(f32[4,768]{1,0:T(4,128)S(1)} %add.128), channel_id=1, source_target_pairs={{0,16},{2,18},{4,20},{6,22},{8,24},{10,26},{12,28},{14,30},{16,0},... | collective-permute-start | bytes 36872 | tf_op jit(solution)/shard_map/ppermute | solution.py:682
  361.9 6.1 %slice-start = ((s8[4718592]{0:T(1024)(128)(4,1)}), s8[4194304]{0:T(1024)(128)(4,1)S(1)}, s32[]{:S(2)}) async-start(s8[4718592]{0:T(1024)(128)(4,1)} %bitcast.62), calls=%async_computation.3 | async-start | bytes 8388608
  362.1 5.8 %slice-start.1 = ((s8[4718592]{0:T(1024)(128)(4,1)}), s8[524288]{0:T(1024)(128)(4,1)S(1)}, s32[]{:S(2)}) async-start(s8[4718592]{0:T(1024)(128)(4,1)} %bitcast.62), calls=%async_computation.4 | async-start | bytes 1048576
  362.1 16.3 %collective-permute-start.16 = (bf16[4,96,768]{2,1,0:T(8,128)(2,1)S(1)}, bf16[4,96,768]{2,1,0:T(8,128)(2,1)S(1)}, u32[]{:S(2)}, u32[]{:S(2)}) collective-permute-start(bf16[4,96,768]{2,1,0:T(8,128)(2,1)S(1)} %get-tuple-element.70), channel_id=1, source_target_pairs={{0,4},{2,6},{4,0},{6,2},{8,12},{10,14},{12,8},{14,10},{16,20},{18,... | collective-permute-start | bytes 1769480 | tf_op jit(solution)/shard_map/ppermute | solution.py:682
  365.6 50.8 %collective-permute-start.23 = (bf16[4,192,768]{2,1,0:T(8,128)(2,1)S(1)}, bf16[4,192,768]{2,1,0:T(8,128)(2,1)S(1)}, u32[]{:S(2)}, u32[]{:S(2)}) collective-permute-start(bf16[4,192,768]{2,1,0:T(8,128)(2,1)S(1)} %get-tuple-element.66), channel_id=1, source_target_pairs={{0,4},{2,6},{4,0},{6,2},{8,12},{10,14},{12,8},{14,10},{16,20},{18,... | collective-permute-start | bytes 3538952 | tf_op jit(solution)/shard_map/ppermute | solution.py:682
  367.0 47.1 %collective-permute-start.12 = (bf16[4,96,768]{2,1,0:T(8,128)(2,1)S(1)}, bf16[4,96,768]{2,1,0:T(8,128)(2,1)S(1)}, u32[]{:S(2)}, u32[]{:S(2)}) collective-permute-start(bf16[4,96,768]{2,1,0:T(8,128)(2,1)S(1)} %get-tuple-element.72), channel_id=1, source_target_pairs={{0,4},{2,6},{4,0},{6,2},{8,12},{10,14},{12,8},{14,10},{16,20},{18,... | collective-permute-start | bytes 1769480 | tf_op jit(solution)/shard_map/ppermute | solution.py:682
  368.5 3.8 collective-permute-start.8
  372.3 45.0 %copy-start.31 = (f32[4,768]{1,0:T(4,128)}, f32[4,768]{1,0:T(4,128)S(1)}, u32[]{:S(2)}) copy-start(f32[4,768]{1,0:T(4,128)S(1)} %add.130) | copy-start | bytes 36868
  379.3 38.7 %collective-permute-start.17 = (bf16[2,96,768]{2,1,0:T(8,128)(2,1)}, bf16[2,96,768]{2,1,0:T(8,128)(2,1)}, u32[]{:S(2)}, u32[]{:S(2)}) collective-permute-start(bf16[2,96,768]{2,1,0:T(8,128)(2,1)} %get-tuple-element.74), channel_id=1, source_target_pairs={{0,8},{2,10},{4,12},{6,14},{8,0},{10,2},{12,4},{14,6},{16,24},{18,... | collective-permute-start | bytes 884744 | tf_op jit(solution)/shard_map/ppermute | solution.py:682
  415.0 14.9 %collective-permute-start.13 = (bf16[2,96,768]{2,1,0:T(8,128)(2,1)}, bf16[2,96,768]{2,1,0:T(8,128)(2,1)}, u32[]{:S(2)}, u32[]{:S(2)}) collective-permute-start(bf16[2,96,768]{2,1,0:T(8,128)(2,1)} %get-tuple-element.76), channel_id=1, source_target_pairs={{0,8},{2,10},{4,12},{6,14},{8,0},{10,2},{12,4},{14,6},{16,24},{18,... | collective-permute-start | bytes 884744 | tf_op jit(solution)/shard_map/ppermute | solution.py:682
  416.5 24.4 %collective-permute-start.24 = (bf16[2,192,768]{2,1,0:T(8,128)(2,1)S(1)}, bf16[2,192,768]{2,1,0:T(8,128)(2,1)S(1)}, u32[]{:S(2)}, u32[]{:S(2)}) collective-permute-start(bf16[2,192,768]{2,1,0:T(8,128)(2,1)S(1)} %get-tuple-element.68), channel_id=1, source_target_pairs={{0,8},{2,10},{4,12},{6,14},{8,0},{10,2},{12,4},{14,6},{16,24},{18,... | collective-permute-start | bytes 1769480 | tf_op jit(solution)/shard_map/ppermute | solution.py:682
  418.9 22.3 %collective-permute-start.18 = (bf16[1,96,768]{2,1,0:T(8,128)(2,1)S(1)}, bf16[1,96,768]{2,1,0:T(8,128)(2,1)S(1)}, u32[]{:S(2)}, u32[]{:S(2)}) collective-permute-start(bf16[1,96,768]{2,1,0:T(8,128)(2,1)S(1)} %fusion.16), channel_id=1, source_target_pairs={{0,16},{2,18},{4,20},{6,22},{8,24},{10,26},{12,28},{14,30},{16,0},... | collective-permute-start | bytes 442376 | tf_op jit(solution)/shard_map/ppermute | solution.py:682
  430.8 12.1 %collective-permute-start.14 = (bf16[1,96,768]{2,1,0:T(8,128)(2,1)S(1)}, bf16[1,96,768]{2,1,0:T(8,128)(2,1)S(1)}, u32[]{:S(2)}, u32[]{:S(2)}) collective-permute-start(bf16[1,96,768]{2,1,0:T(8,128)(2,1)S(1)} %fusion.19), channel_id=1, source_target_pairs={{0,16},{2,18},{4,20},{6,22},{8,24},{10,26},{12,28},{14,30},{16,0},... | collective-permute-start | bytes 442376 | tf_op jit(solution)/shard_map/ppermute | solution.py:682
  441.0 13.7 %collective-permute-start.25 = (bf16[1,192,768]{2,1,0:T(8,128)(2,1)S(1)}, bf16[1,192,768]{2,1,0:T(8,128)(2,1)S(1)}, u32[]{:S(2)}, u32[]{:S(2)}) collective-permute-start(bf16[1,192,768]{2,1,0:T(8,128)(2,1)S(1)} %fusion.11), channel_id=1, source_target_pairs={{0,16},{2,18},{4,20},{6,22},{8,24},{10,26},{12,28},{14,30},{16,0},... | collective-permute-start | bytes 884744 | tf_op jit(solution)/shard_map/ppermute | solution.py:682
  441.2 14.3 %copy-start.1 = (f32[12,32]{1,0:T(8,128)S(1)}, f32[12,32]{1,0:T(8,128)}, u32[]{:S(2)}) copy-start(f32[12,32]{1,0:T(8,128)} %param.17) | copy-start | bytes 4612
  (18 other events, 56.7 us)
Sparse Core Ops, SparseCore 0:
  10.3 55.8 all-gather.4
  68.5 51.6 all-gather.6
  122.5 79.4 all-gather.8
